TPU v7x, 32 devices: a whole 2x2x4 slice. The times are simulated.
32 devices in a mesh: ctx: 8 (over z, y), head: 4 (over x, core).
Axes of the slice: x: 2, y: 2, z: 4, core: 2. Of those that a mesh axis runs over, the one named last changes fastest.
Arguments:
- x_in: bfloat16 [4096, 1024], P(('ctx', 'head')), may hold values from -6 to 6
- in_weight: bfloat16 [1024, 4120], P(('ctx', 'head')), may hold values from -1 to 1
- out_weight: bfloat16 [2048, 1024], P(('ctx', 'head')), may hold values from -0.1875 to 0.1875
- gu_weight: bfloat16 [1024, 4096], P(('ctx', 'head')), may hold values from -0.1875 to 0.1875
- down_weight: bfloat16 [2048, 1024], P(('ctx', 'head')), may hold values from -0.125 to 0.125
- norm_gain: bfloat16 [1024], P(('ctx', 'head')), may hold values from 0.5 to 1.5
- mixer_gain: bfloat16 [1536], P(('ctx', 'head')), may hold values from 0.5 to 1.5
- ffn_gain: bfloat16 [1024], P(('ctx', 'head')), may hold values from 0.5 to 1.5
- conv_weight: bfloat16 [1792, 4], P(('ctx', 'head')), may hold values from -3 to 3
- conv_bias: bfloat16 [1792], P(('ctx', 'head')), may hold values from -3 to 3
- dt_bias: float32 [24], P('head'), may hold values from -1 to 1
- a_log: float32 [24], P('head'), may hold values from -14 to -2
- skip_gain: float32 [24], P('head'), may hold values from 0 to 2
- out_grad: bfloat16 [4096, 1024], P(('ctx', 'head')), may hold values from -6 to 6
Outputs:
- y_out: bfloat16 [4096, 1024], P(('ctx', 'head'))
- x_grad: float32 [4096, 1024], P(('ctx', 'head'))
- in_weight_grad: float32 [1024, 4120], P(('ctx', 'head'))
- out_weight_grad: float32 [2048, 1024], P(('ctx', 'head'))
- gu_weight_grad: float32 [1024, 4096], P(('ctx', 'head'))
- down_weight_grad: float32 [2048, 1024], P(('ctx', 'head'))
- norm_gain_grad: float32 [1024], P(('ctx', 'head'))
- mixer_gain_grad: float32 [1536], P(('ctx', 'head'))
- ffn_gain_grad: float32 [1024], P(('ctx', 'head'))
- conv_weight_grad: float32 [1792, 4], P(('ctx', 'head'))
- conv_bias_grad: float32 [1792], P(('ctx', 'head'))
- dt_bias_grad: float32 [24], P('head')
- a_log_grad: float32 [24], P('head')
- skip_grad: float32 [24], P('head')
All inputs are finite; a program needn't handle non-finite values.
Results may differ from a plain program's by a relative error of at most 0.018.
The roundings to bfloat16 on the way count: a program that leaves them out, or rounds other values in their place, can miss the bound.
Values may be sent and summed in bfloat16 or wider, within the bound.
A program may use at most 192 MiB of HBM per device.

v0:
```python
import math

import jax
import jax.numpy as jnp
from jax import lax
from jax.sharding import PartitionSpec as P

FF = 2048
MH = 24
MP = 64
NS = 128
KW = 4
AH = 8
KVH = 2
HDIM = 64
SB = 256


EPSILON = 1e-05
ROPE_BASE = 10000.0
PRECISE_MODE = lax.Precision.HIGHEST


def passed_along(block, axis, distance):
    devices = range(lax.axis_size(axis))
    route = [(i - distance, i) for i in devices if i - distance in devices]
    return lax.ppermute(block, axis, route)


def prefix(part, axis, combine, identity):
    place = lax.axis_index(axis)
    gathered = jax.tree.map(lambda a: lax.all_gather(a, axis), part)
    state = jax.tree.map(lambda a, e: jnp.zeros_like(a) + jnp.asarray(e, a.dtype), part, identity)

    def one(hop, state):
        return combine(
            state, jax.tree.map(lambda a: lax.dynamic_index_in_dim(a, hop, 0, False), gathered)
        )

    return lax.fori_loop(0, place, one, state)


def carried_in(array, axis, combine, identity):
    peers, index = (lax.axis_size(axis), lax.axis_index(axis))
    everything = jax.tree.map(
        lambda part, kind: lax.all_gather(part.astype(kind), axis),
        array,
        (jnp.bfloat16, jnp.bfloat16),
    )
    start = jax.tree.map(
        lambda part, zero: jnp.broadcast_to(jnp.asarray(zero, part.dtype), part.shape),
        array,
        identity,
    )

    def hop(k, before):
        at = peers - 1 - k
        reached = at > index
        new = combine(
            before, jax.tree.map(lambda part, own: part[at].astype(own.dtype), everything, array)
        )
        return jax.tree.map(lambda a, b: jnp.where(reached, a, b), new, before)

    return lax.fori_loop(0, peers, hop, start)


def silu_grad(value):
    sigmoid = jax.nn.sigmoid(value)
    return sigmoid * (1.0 + value * (1.0 - sigmoid))


def rotate_pairs(values, positions, direction):
    half_dim = values.shape[-1] // 2
    inverse = ROPE_BASE ** (-jnp.arange(half_dim).astype(jnp.float32) / half_dim)
    angles = positions[:, None] * inverse[None, :]
    cosine = jnp.cos(angles)[:, None, :]
    sine = direction * jnp.sin(angles)[:, None, :]
    first_half = values[..., :half_dim]
    second_half = values[..., half_dim:]
    return jnp.concatenate(
        [first_half * cosine - second_half * sine, second_half * cosine + first_half * sine],
        axis=-1,
    )


def state_block(state, pieces, decay_rate, skip_gain):
    inputs_x, bmat, cmat, step_size = pieces
    length = inputs_x.shape[0]
    cumulative = jnp.cumsum(step_size * decay_rate[None, :], axis=0)
    lower = (jnp.arange(length)[:, None] >= jnp.arange(length)[None, :])[None, :, :]
    spread = cumulative.T[:, :, None] - cumulative.T[:, None, :]
    within = jnp.where(lower, jnp.exp(jnp.where(lower, spread, 0.0)), 0.0)
    scaled_x = inputs_x * step_size[:, :, None]
    products = jnp.dot(cmat, bmat.T, precision=PRECISE_MODE)
    intra = jnp.einsum("ts,hts,shp->thp", products, within, scaled_x, precision=PRECISE_MODE)
    inter = (
        jnp.einsum("tn,hpn->thp", cmat, state, precision=PRECISE_MODE)
        * jnp.exp(cumulative)[:, :, None]
    )
    remain = jnp.exp(cumulative[-1][None, :] - cumulative)
    new_state = jnp.exp(cumulative[-1])[:, None, None] * state + jnp.einsum(
        "sh,shp,sn->hpn", remain, scaled_x, bmat, precision=PRECISE_MODE
    )
    return (new_state, intra + inter + skip_gain[None, :, None] * inputs_x)


def mixer_local(inputs_x, bmat, cmat, step_size, decay_rate, skip_gain, state):
    count = inputs_x.shape[0] // SB

    def advance(carry, pieces):
        return state_block(carry, pieces, decay_rate, skip_gain)

    def shaped(value):
        return value.reshape((count, SB) + value.shape[1:])

    final, outputs = lax.scan(
        advance, state, (shaped(inputs_x), shaped(bmat), shaped(cmat), shaped(step_size))
    )
    return (outputs.reshape(inputs_x.shape), final)


def chain_combine(earlier, later):
    return (earlier[0] * later[0], later[0][:, None, None] * earlier[1] + later[1])


def dot_back(first_op, second_op):
    return lax.dot_general(
        first_op, second_op, (((1,), (1,)), ((), ())), preferred_element_type=jnp.float32
    )


def dot_rows(first_op, second_op):
    return lax.dot_general(
        first_op, second_op, (((0,), (0,)), ((), ())), preferred_element_type=jnp.float32
    )


def block_scores(queries, keys, query_first, key_first):
    raw = jnp.einsum("thd,ud->thu", queries, keys, preferred_element_type=jnp.float32) * (
        1.0 / math.sqrt(HDIM)
    )
    valid = (key_first + jnp.arange(keys.shape[0]))[None, None, :] <= (
        query_first + jnp.arange(queries.shape[0])
    )[:, None, None]
    return jnp.where(valid, raw, -jnp.inf)


def on_device(
    x_in,
    in_weight,
    out_weight,
    gu_weight,
    down_weight,
    norm_gain,
    mixer_gain,
    ffn_gain,
    conv_weight,
    conv_bias,
    dt_bias,
    a_log,
    skip_gain,
    out_grad,
):
    float_type = jnp.float32
    half_type = jnp.bfloat16
    head_count = lax.axis_size("head")
    ctx_count = lax.axis_size("ctx")
    ctx_place = lax.axis_index("ctx")
    head_place = lax.axis_index("head")
    tokens = x_in.shape[0]
    seq_rows = tokens * head_count
    mix_heads = MH // head_count
    attn_heads = AH // head_count
    group_devices = head_count // KVH
    dssm_cols = MH * MP
    conv_cols = dssm_cols + 2 * NS
    mine_cols = mix_heads * MP
    local_cols = mine_cols + 2 * NS
    query_start = 2 * dssm_cols + 2 * NS + MH
    key_start = query_start + AH * HDIM
    value_start = key_start + KVH * HDIM
    score_scale = 1.0 / math.sqrt(HDIM)
    w_in, w_out, w_gu, w_down, gain_one, gain_mix, gain_two, conv_w, conv_b = (
        lax.all_gather(in_weight, ("ctx", "head"), axis=0, tiled=True),
        lax.all_gather(out_weight, ("ctx", "head"), axis=0, tiled=True),
        lax.all_gather(gu_weight, ("ctx", "head"), axis=0, tiled=True),
        lax.all_gather(down_weight, ("ctx", "head"), axis=0, tiled=True),
        lax.all_gather(norm_gain, ("ctx", "head"), axis=0, tiled=True),
        lax.all_gather(mixer_gain, ("ctx", "head"), axis=0, tiled=True),
        lax.all_gather(ffn_gain, ("ctx", "head"), axis=0, tiled=True),
        lax.all_gather(conv_weight, ("ctx", "head"), axis=0, tiled=True),
        lax.all_gather(conv_bias, ("ctx", "head"), axis=0, tiled=True),
    )
    gain_one = gain_one.astype(float_type)
    gain_mix = gain_mix.astype(float_type)
    gain_two = gain_two.astype(float_type)
    inputs = x_in.astype(float_type)
    rms_in = lax.rsqrt(jnp.mean(inputs * inputs, axis=1, keepdims=True) + EPSILON)
    normed = (inputs * rms_in * gain_one[None, :]).astype(half_type)
    proj = jnp.dot(normed, w_in, preferred_element_type=float_type).astype(half_type)
    sends = []
    rates = []
    for target in range(head_count):
        kv_index = target // group_devices
        sends.append(
            jnp.concatenate(
                [
                    proj[:, dssm_cols + target * mine_cols : dssm_cols + (target + 1) * mine_cols],
                    proj[:, 2 * dssm_cols : 2 * dssm_cols + 2 * NS],
                    proj[
                        :,
                        query_start
                        + target * attn_heads * HDIM : query_start
                        + (target + 1) * attn_heads * HDIM,
                    ],
                    proj[:, key_start + kv_index * HDIM : key_start + (kv_index + 1) * HDIM],
                    proj[:, value_start + kv_index * HDIM : value_start + (kv_index + 1) * HDIM],
                ],
                axis=1,
            )
        )
        rates.append(
            proj[
                :,
                dssm_cols
                + conv_cols
                + target * mix_heads : dssm_cols
                + conv_cols
                + (target + 1) * mix_heads,
            ]
        )
    arrived, rate_raw = (
        lax.all_to_all(jnp.stack(sends), "head", split_axis=0, concat_axis=1, tiled=True),
        lax.all_to_all(jnp.stack(rates), "head", split_axis=0, concat_axis=1, tiled=True),
    )
    arrived = arrived[0]
    rate_raw = rate_raw[0]
    xbc = arrived[:, :local_cols]
    queries_raw = arrived[:, local_cols : local_cols + attn_heads * HDIM]
    keys_raw = arrived[:, local_cols + attn_heads * HDIM : local_cols + attn_heads * HDIM + HDIM]
    values_raw = arrived[:, local_cols + attn_heads * HDIM + HDIM :]
    rim = passed_along(xbc[seq_rows - (KW - 1) :], "ctx", 1)
    padded = jnp.concatenate([rim, xbc], axis=0).astype(float_type)
    own_w = jnp.concatenate(
        [
            lax.dynamic_slice_in_dim(conv_w, head_place * mine_cols, mine_cols, 0),
            conv_w[dssm_cols:],
        ],
        axis=0,
    ).astype(float_type)
    own_b = jnp.concatenate(
        [
            lax.dynamic_slice_in_dim(conv_b, head_place * mine_cols, mine_cols, 0),
            conv_b[dssm_cols:],
        ],
        axis=0,
    ).astype(float_type)
    conv_pre = jnp.broadcast_to(own_b[None, :], (seq_rows, local_cols))
    for offset in range(KW):
        conv_pre = conv_pre + padded[offset : offset + seq_rows] * own_w[:, offset][None, :]
    conv_out = jax.nn.silu(conv_pre).astype(half_type)
    mix_x = conv_out[:, :mine_cols].astype(float_type).reshape(seq_rows, mix_heads, MP)
    bmat = conv_out[:, mine_cols : mine_cols + NS].astype(float_type)
    cmat = conv_out[:, mine_cols + NS :].astype(float_type)
    dt_pre = rate_raw.astype(float_type) + dt_bias[None, :]
    step_size = jax.nn.softplus(dt_pre)
    decay_rate = -jnp.exp(a_log)
    zero_state = jnp.zeros((mix_heads, MP, NS), float_type)
    ssm_zero, ends = mixer_local(mix_x, bmat, cmat, step_size, decay_rate, skip_gain, zero_state)
    cumall = jnp.cumsum(step_size * decay_rate[None, :], axis=0)
    stretch_decay = jnp.exp(cumall[-1])
    carry_in = prefix(
        (stretch_decay, ends),
        "ctx",
        chain_combine,
        (jnp.ones_like(stretch_decay), jnp.zeros_like(ends)),
    )[1]
    ssm_full = ssm_zero + jnp.exp(cumall)[:, :, None] * jnp.einsum(
        "tn,hpn->thp", cmat, carry_in, precision=PRECISE_MODE
    )
    ssm_send = ssm_full.reshape(seq_rows, mine_cols).astype(half_type)
    query_first = ctx_place * seq_rows
    positions = (query_first + jnp.arange(seq_rows)).astype(float_type)
    q_rot = rotate_pairs(
        queries_raw.astype(float_type).reshape(seq_rows, attn_heads, HDIM), positions, 1.0
    ).astype(half_type)
    k_rot = (
        rotate_pairs(keys_raw.astype(float_type).reshape(seq_rows, 1, HDIM), positions, 1.0)
        .reshape(seq_rows, HDIM)
        .astype(half_type)
    )
    kv_all = lax.all_gather(jnp.concatenate([k_rot, values_raw], axis=1), "ctx", axis=0, tiled=True)

    def key_slice(number):
        piece = lax.dynamic_slice_in_dim(kv_all, number * seq_rows, seq_rows, 0)
        return (piece[:, :HDIM], piece[:, HDIM:])

    def stat_step(number, carry):
        row_peak, row_mass = carry
        keys_blk = key_slice(number)[0]
        scores = block_scores(q_rot, keys_blk, query_first, number * seq_rows)
        new_peak = jnp.maximum(row_peak, jnp.max(scores, axis=2))
        row_mass = row_mass * jnp.exp(row_peak - new_peak) + jnp.sum(
            jnp.exp(scores - new_peak[:, :, None]), axis=2
        )
        return (new_peak, row_mass)

    row_peak, row_mass = lax.fori_loop(
        0,
        ctx_place + 1,
        stat_step,
        (
            jnp.full((seq_rows, attn_heads), -jnp.inf, float_type),
            jnp.zeros((seq_rows, attn_heads), float_type),
        ),
    )
    log_total = row_peak + jnp.log(row_mass)

    def out_step(number, accum):
        keys_blk, vals_blk = key_slice(number)
        probs = jnp.exp(
            block_scores(q_rot, keys_blk, query_first, number * seq_rows) - log_total[:, :, None]
        ).astype(half_type)
        return accum + jnp.einsum("thu,ud->thd", probs, vals_blk, preferred_element_type=float_type)

    attn_out = lax.fori_loop(
        0, ctx_place + 1, out_step, jnp.zeros((seq_rows, attn_heads, HDIM), float_type)
    ).astype(half_type)
    ssm_tok, attn_tok = (
        lax.all_to_all(ssm_send, "head", split_axis=0, concat_axis=1, tiled=True),
        lax.all_to_all(
            attn_out.reshape(seq_rows, attn_heads * HDIM),
            "head",
            split_axis=0,
            concat_axis=1,
            tiled=True,
        ),
    )
    z_part = proj[:, :dssm_cols].astype(float_type)
    ssm_tok_f = ssm_tok.astype(float_type)
    gated = ssm_tok_f * jax.nn.silu(z_part)
    rms_mix = lax.rsqrt(jnp.mean(gated * gated, axis=1, keepdims=True) + EPSILON)
    mixed_norm = (gated * rms_mix * gain_mix[None, :]).astype(half_type)
    joined = jnp.concatenate([mixed_norm, attn_tok], axis=1)
    residual = inputs + jnp.dot(joined, w_out, preferred_element_type=float_type)
    rms_ffn = lax.rsqrt(jnp.mean(residual * residual, axis=1, keepdims=True) + EPSILON)
    normed_ffn = (residual * rms_ffn * gain_two[None, :]).astype(half_type)
    gate_up = jnp.dot(normed_ffn, w_gu, preferred_element_type=float_type)
    gate_part = gate_up[:, :FF]
    up_part = gate_up[:, FF:]
    activ = (jax.nn.silu(gate_part) * up_part).astype(half_type)
    y_out = (residual + jnp.dot(activ, w_down, preferred_element_type=float_type)).astype(half_type)
    d_activ = dot_back(out_grad, w_down)
    down_grad = dot_rows(activ, out_grad)
    d_gate_up = jnp.concatenate(
        [d_activ * up_part * silu_grad(gate_part), d_activ * jax.nn.silu(gate_part)], axis=1
    ).astype(half_type)
    d_normed_ffn = dot_back(d_gate_up, w_gu)
    gu_grad = dot_rows(normed_ffn, d_gate_up)
    ffn_gain_grad = jnp.sum(d_normed_ffn * residual * rms_ffn, axis=0)
    scaled_ffn = gain_two[None, :] * d_normed_ffn
    d_residual = (
        out_grad.astype(float_type)
        + rms_ffn * scaled_ffn
        - residual * rms_ffn**3 * jnp.mean(scaled_ffn * residual, axis=1, keepdims=True)
    )
    d_res_half = d_residual.astype(half_type)
    d_joined = dot_back(d_res_half, w_out)
    out_weight_grad = dot_rows(joined, d_res_half)
    d_mixed = d_joined[:, :dssm_cols]
    d_attn_tok = d_joined[:, dssm_cols:].astype(half_type)
    mixer_gain_grad = jnp.sum(d_mixed * gated * rms_mix, axis=0)
    scaled_mix = gain_mix[None, :] * d_mixed
    d_gated = rms_mix * scaled_mix - gated * rms_mix**3 * jnp.mean(
        scaled_mix * gated, axis=1, keepdims=True
    )
    d_ssm_tok = (d_gated * jax.nn.silu(z_part)).astype(half_type)
    d_z = d_gated * ssm_tok_f * silu_grad(z_part)
    d_ssm_head, d_attn_head = (
        lax.all_to_all(d_ssm_tok, "head", split_axis=1, concat_axis=0, tiled=True),
        lax.all_to_all(d_attn_tok, "head", split_axis=1, concat_axis=0, tiled=True),
    )
    d_out3 = d_attn_head.reshape(seq_rows, attn_heads, HDIM)
    row_delta = jnp.sum(d_out3.astype(float_type) * attn_out.astype(float_type), axis=2)

    def back_step(number, carry):
        query_grad, kv_grads = carry
        keys_blk, vals_blk = key_slice(number)
        probs = jnp.exp(
            block_scores(q_rot, keys_blk, query_first, number * seq_rows) - log_total[:, :, None]
        )
        d_probs = jnp.einsum("thd,ud->thu", d_out3, vals_blk, preferred_element_type=float_type)
        d_scores = (probs * (d_probs - row_delta[:, :, None])).astype(half_type)
        query_grad = (
            query_grad
            + jnp.einsum("thu,ud->thd", d_scores, keys_blk, preferred_element_type=float_type)
            * score_scale
        )
        key_part = (
            jnp.einsum("thu,thd->ud", d_scores, q_rot, preferred_element_type=float_type)
            * score_scale
        )
        value_part = jnp.einsum(
            "thu,thd->ud", probs.astype(half_type), d_out3, preferred_element_type=float_type
        )
        kv_grads = lax.dynamic_update_slice_in_dim(
            kv_grads, jnp.concatenate([key_part, value_part], axis=1), number * seq_rows, 0
        )
        return (query_grad, kv_grads)

    query_grad, kv_grads = lax.fori_loop(
        0,
        ctx_place + 1,
        back_step,
        (jnp.zeros((seq_rows, attn_heads, HDIM), float_type), jnp.zeros(kv_all.shape, float_type)),
    )
    d_ssm3 = d_ssm_head.astype(float_type).reshape(seq_rows, mix_heads, MP)
    local_pull = jnp.einsum("th,thp,tn->hpn", jnp.exp(cumall), d_ssm3, cmat, precision=PRECISE_MODE)
    d_end = carried_in(
        (stretch_decay, local_pull),
        "ctx",
        chain_combine,
        (jnp.ones_like(stretch_decay), jnp.zeros_like(local_pull)),
    )[1]

    def run_local(mix_in, b_in, c_in, step_in, decay_in, skip_in):
        return mixer_local(mix_in, b_in, c_in, step_in, decay_in, skip_in, carry_in)

    recomputed, pullback = jax.vjp(run_local, mix_x, bmat, cmat, step_size, decay_rate, skip_gain)
    grad_x, grad_b, grad_c, grad_step, grad_decay, skip_part = pullback((d_ssm3, d_end))
    d_dt_pre = grad_step * jax.nn.sigmoid(dt_pre)
    head_local = jnp.stack([jnp.sum(d_dt_pre, axis=0), grad_decay * decay_rate, skip_part])
    head_tiled = jnp.broadcast_to(head_local[None], (ctx_count, 3, mix_heads))
    kv_mine, head_sums = (
        lax.psum_scatter(
            kv_grads.astype(jnp.bfloat16), "ctx", scatter_dimension=0, tiled=True
        ).astype(jnp.float32),
        lax.psum_scatter(
            head_tiled.astype(jnp.bfloat16), "ctx", scatter_dimension=0, tiled=True
        ).astype(jnp.float32),
    )
    head_sums = head_sums[0]
    d_query = rotate_pairs(query_grad, positions, -1.0).reshape(seq_rows, attn_heads * HDIM)
    d_key = rotate_pairs(kv_mine[:, None, :HDIM], positions, -1.0).reshape(seq_rows, HDIM)
    d_value = kv_mine[:, HDIM:]
    d_conv_pre = jnp.concatenate(
        [grad_x.reshape(seq_rows, mine_cols), grad_b, grad_c], axis=1
    ) * silu_grad(conv_pre)
    conv_b_local = jnp.sum(d_conv_pre, axis=0)
    conv_w_local = jnp.stack(
        [jnp.sum(d_conv_pre * padded[offset : offset + seq_rows], axis=0) for offset in range(KW)],
        axis=1,
    )
    d_padded = jnp.zeros((seq_rows + KW - 1, local_cols), float_type)
    for offset in range(KW):
        d_padded = d_padded + jnp.pad(
            d_conv_pre * own_w[:, offset][None, :], ((offset, KW - 1 - offset), (0, 0))
        )
    rim_back = passed_along(d_padded[: KW - 1], "ctx", -1)
    d_xbc = d_padded[KW - 1 :] + jnp.pad(rim_back, ((seq_rows - (KW - 1), 0), (0, 0)))
    conv_w_full = jnp.zeros((conv_cols, KW), float_type)
    conv_w_full = lax.dynamic_update_slice_in_dim(
        conv_w_full, conv_w_local[:mine_cols], head_place * mine_cols, 0
    )
    conv_w_full = lax.dynamic_update_slice_in_dim(
        conv_w_full, conv_w_local[mine_cols:], dssm_cols, 0
    )
    conv_b_full = jnp.zeros((conv_cols,), float_type)
    conv_b_full = lax.dynamic_update_slice_in_dim(
        conv_b_full, conv_b_local[:mine_cols], head_place * mine_cols, 0
    )
    conv_b_full = lax.dynamic_update_slice_in_dim(
        conv_b_full, conv_b_local[mine_cols:], dssm_cols, 0
    )
    back_main = jnp.concatenate([d_xbc, d_query, d_key, d_value], axis=1)
    got_main, got_rates = (
        lax.all_to_all(
            back_main.astype(jnp.bfloat16), "head", split_axis=0, concat_axis=1, tiled=True
        ).astype(back_main.dtype),
        lax.all_to_all(
            d_dt_pre.astype(jnp.bfloat16), "head", split_axis=0, concat_axis=1, tiled=True
        ).astype(d_dt_pre.dtype),
    )
    per_source = got_main.reshape(tokens, head_count, local_cols + attn_heads * HDIM + 2 * HDIM)
    d_x_all = per_source[:, :, :mine_cols].reshape(tokens, dssm_cols)
    d_b_all = jnp.sum(per_source[:, :, mine_cols : mine_cols + NS], axis=1)
    d_c_all = jnp.sum(per_source[:, :, mine_cols + NS : local_cols], axis=1)
    key_col = local_cols + attn_heads * HDIM
    d_q_all = per_source[:, :, local_cols:key_col].reshape(tokens, AH * HDIM)
    d_k_all = jnp.sum(
        per_source[:, :, key_col : key_col + HDIM].reshape(tokens, KVH, group_devices, HDIM), axis=2
    ).reshape(tokens, KVH * HDIM)
    d_v_all = jnp.sum(
        per_source[:, :, key_col + HDIM :].reshape(tokens, KVH, group_devices, HDIM), axis=2
    ).reshape(tokens, KVH * HDIM)
    d_proj = jnp.concatenate(
        [d_z, d_x_all, d_b_all, d_c_all, got_rates, d_q_all, d_k_all, d_v_all], axis=1
    ).astype(half_type)
    d_normed = dot_back(d_proj, w_in)
    in_grad = dot_rows(normed, d_proj)
    norm_gain_grad = jnp.sum(d_normed * inputs * rms_in, axis=0)
    scaled_in = gain_one[None, :] * d_normed
    x_grad = (
        d_residual
        + rms_in * scaled_in
        - inputs * rms_in**3 * jnp.mean(scaled_in * inputs, axis=1, keepdims=True)
    )
    (
        input_sum,
        output_sum,
        gate_sum,
        down_sum,
        norm_sum,
        mixer_sum,
        feed_sum,
        conv_weight_sum,
        conv_bias_sum,
    ) = (
        lax.psum_scatter(in_grad, ("ctx", "head"), scatter_dimension=0, tiled=True),
        lax.psum_scatter(out_weight_grad, ("ctx", "head"), scatter_dimension=0, tiled=True),
        lax.psum_scatter(gu_grad, ("ctx", "head"), scatter_dimension=0, tiled=True),
        lax.psum_scatter(down_grad, ("ctx", "head"), scatter_dimension=0, tiled=True),
        lax.psum_scatter(norm_gain_grad, ("ctx", "head"), scatter_dimension=0, tiled=True),
        lax.psum_scatter(mixer_gain_grad, ("ctx", "head"), scatter_dimension=0, tiled=True),
        lax.psum_scatter(ffn_gain_grad, ("ctx", "head"), scatter_dimension=0, tiled=True),
        lax.psum_scatter(conv_w_full, ("ctx", "head"), scatter_dimension=0, tiled=True),
        lax.psum_scatter(conv_b_full, ("ctx", "head"), scatter_dimension=0, tiled=True),
    )
    return (
        y_out,
        x_grad,
        input_sum,
        output_sum,
        gate_sum,
        down_sum,
        norm_sum,
        mixer_sum,
        feed_sum,
        conv_weight_sum,
        conv_bias_sum,
        head_sums[0],
        head_sums[1],
        head_sums[2],
    )


def solution(mesh):
    placed = (
        P(("ctx", "head"), None),
        P(("ctx", "head"), None),
        P(("ctx", "head"), None),
        P(("ctx", "head"), None),
        P(("ctx", "head"), None),
        P(("ctx", "head")),
        P(("ctx", "head")),
        P(("ctx", "head")),
        P(("ctx", "head"), None),
        P(("ctx", "head")),
        P("head"),
        P("head"),
        P("head"),
        P(("ctx", "head"), None),
    )
    return jax.shard_map(
        on_device,
        mesh=mesh,
        in_specs=placed,
        out_specs=(
            P(("ctx", "head"), None),
            P(("ctx", "head"), None),
            P(("ctx", "head"), None),
            P(("ctx", "head"), None),
            P(("ctx", "head"), None),
            P(("ctx", "head"), None),
            P(("ctx", "head")),
            P(("ctx", "head")),
            P(("ctx", "head")),
            P(("ctx", "head"), None),
            P(("ctx", "head")),
            P("head"),
            P("head"),
            P("head"),
        ),
        check_vma=False,
    )
```

profile of v0, /device:TPU:0, one launch (start us, length us, event | category | flops | bytes accessed | tf_op | source)
XLA Modules:
  0.0 1286.3 jit_solution(6717574251922999010)
XLA Ops:
  11.3 43.5 %all-reduce.18 = (bf16[1024]{0:T(1024)(128)(2,1)S(1)}, bf16[1536]{0:T(1024)(128)(2,1)S(1)}, bf16[1792]{0:T(1024)(128)(2,1)S(1)}, bf16[1024]{0:T(1024)(128)(2,1)S(1)}) all-reduce(bf16[1024]{0:T(1024)(128)(2,1)S(1)} %dynamic-update-slice, bf16[1536]{0:T(1024)(128)(2,1)S(1)} %dynamic-update-slice.2, ...), channel_id=1, replica_groups=mesh['ctx'=8,'head'=4] {'ctx','head'}, use_global_device_ids=true, to_apply=%add.7 | all-reduce | flops 5376 | bytes 21504
  54.8 40.7 %all-gather.2 = bf16[32,56,4]{1,2,0:T(4,128)(2,1)S(1)} all-gather(bf16[1,56,4]{1,2,0:T(4,128)(2,1)} %bitcast.854), channel_id=1, replica_groups=mesh['ctx'=8,'head'=4] {'ctx','head'}, dimensions={0}, use_global_device_ids=true | all-gather | bytes 14784 | tf_op jit(solution)/shard_map/all_gather | solution.py:191
  97.5 7.1 convolution_convert_fusion
  112.5 4.2 all-to-all-start.1
  118.0 11.8 all-to-all-done.1
  149.0 39.1 %while.153 = (s32[]{:T(128)}, f32[6,64,128]{2,1,0:T(8,128)S(1)}, f32[2,256,6,64]{1,0,3,2:T(2,128)}, f32[2,256,6]{1,2,0:T(8,128)S(1)}, f32[6]{0:T(128)S(1)}, /*in...) while((s32[]{:T(128)}, f32[6,64,128]{2,1,0:T(8,128)S(1)}, ...), condition=%wide.region_4.5_spmd.clone, body=%wide.region_1.4_spmd.clone.sunk | while | flops 707365888 | bytes 5835627 | solution.py:116
  159.7 9.0 dynamic_update_slice.250
  179.2 9.0 dynamic_update_slice.250
  194.7 17.7 %all-gather.3 = f32[8,1,6]{2,1,0:T(1,128)S(1)} all-gather(f32[1,1,6]{2,1,0:T(1,128)S(1)} %bitcast.853), channel_id=1, replica_groups=mesh['ctx'=8,'head'=4] {'ctx'}, dimensions={0}, use_global_device_ids=true | all-gather | bytes 216 | tf_op jit(solution)/shard_map/all_gather | solution.py:32
  219.2 11.2 all-gather.22.cloned.1.call-done
  233.1 3.5 all-to-all-start.2
  241.1 3.8 all-to-all-done.2
  244.9 3.7 all-to-all-start.3
  250.5 42.8 %all-gather.16.cloned.1.call-done = bf16[2048,1024]{1,0:T(8,128)(2,1)} async-done(((bf16[64,1024]{1,0:T(8,128)(2,1)}), bf16[2048,1024]{1,0:T(8,128)(2,1)}) %all-gather.16.cloned.1.call-update) | async-done | bytes 4194320 | tf_op jit(solution)/shard_map/all_gather | solution.py:185
  297.1 74.7 %all-gather.18.cloned.1.call-done = bf16[1024,4096]{1,0:T(8,128)(2,1)} async-done(((bf16[32,4096]{1,0:T(8,128)(2,1)}), bf16[1024,4096]{1,0:T(8,128)(2,1)}) %all-gather.18.cloned.1.call-update) | async-done | bytes 8388624 | tf_op jit(solution)/shard_map/all_gather | solution.py:186
  371.8 6.0 fusion.233
  377.8 57.1 %all-gather.20.cloned.1.call-done = bf16[2048,1024]{1,0:T(8,128)(2,1)} async-done(((bf16[64,1024]{1,0:T(8,128)(2,1)}), bf16[2048,1024]{1,0:T(8,128)(2,1)}) %all-gather.20.cloned.1.call-update) | async-done | bytes 4194320 | tf_op jit(solution)/shard_map/all_gather | solution.py:187
  434.9 5.4 multiply_convert_fusion.2
  440.3 3.5 multiply_reduce_fusion.8
  450.6 4.5 all-to-all-done.5
  458.8 8.8 while.151
  467.7 5.8 fusion.192
  475.1 81.1 %all-gather.4 = bf16[8,1,6]{2,1,0:T(2,128)(2,1)S(1)} all-gather(bf16[1,1,6]{2,1,0:T(2,128)(2,1)S(1)} %bitcast.852), channel_id=1, replica_groups=mesh['ctx'=8,'head'=4] {'ctx'}, dimensions={0}, use_global_device_ids=true | all-gather | bytes 108 | tf_op jit(solution)/shard_map/all_gather | solution.py:46
  558.1 39.9 %while.152 = (s32[]{:T(128)}, f32[6,64,128]{2,1,0:T(8,128)S(1)}, f32[2,6,256,256]{3,2,1,0:T(8,128)}, f32[2,256,6,1]{1,2,3,0:T(8,128)}, f32[2,128,256]{1,2,0:T(8,...) while((s32[]{:T(128)}, f32[6,64,128]{2,1,0:T(8,128)S(1)}, ...), condition=%wide.region_24.25_spmd.clone.clone, body=%wide.region_21.24_spmd.clone.clone.sunk | while | flops 406195200 | bytes 9657417 | solution.py:116
  606.5 3.5 all-to-all-start.4
  610.0 5.5 fusion.240
  617.3 4.0 all-to-all-done.4
  625.4 34.0 %all-gather.1 = bf16[48,64,128]{2,1,0:T(8,128)(2,1)S(1)} all-gather(bf16[6,64,128]{2,1,0:T(8,128)(2,1)S(1)} %convolution_convert_fusion.1), channel_id=3, replica_groups=mesh['ctx'=8,'head'=4] {'ctx'}, dimensions={0}, use_global_device_ids=true | all-gather | bytes 884736 | tf_op jit(solution)/shard_map/all_gather | solution.py:46
  659.4 6.5 while.154
  669.0 110.6 %while.155 = (s32[]{:T(128)}, f32[6]{0:T(128)}, f32[6]{0:T(128)}, f32[6,64,128]{2,1,0:T(8,128)S(1)}, f32[2,256,6,64]{1,0,3,2:T(2,128)}, /*index=5*/f32[2,256,128...) while((s32[]{:T(128)}, f32[6]{0:T(128)}, f32[6]{0:T(128)}, ...), condition=%wide.region_36.37_spmd.clone.clone, body=%wide.region_25.36_spmd.clone.clone.sunk | while | flops 1414315008 | bytes 45149572 | solution.py:116
  670.6 4.1 fusion.373
  678.4 3.6 fusion.375
  691.6 7.5 reduce-window.78
  707.0 9.0 dynamic_update_slice.254
  725.5 4.1 fusion.373
  733.3 3.6 fusion.375
  746.5 7.5 reduce-window.78
  762.7 9.0 dynamic_update_slice.254
  795.7 3.5 all-to-all-start.6
  799.3 22.5 %all-to-all-done.6 = bf16[4,128,896]{1,2,0:T(8,128)(2,1)S(1)} async-done(((bf16[4,128,896]{1,2,0:T(8,128)(2,1)}), bf16[4,128,896]{1,2,0:T(8,128)(2,1)S(1)}, u32[]{:S(2)}, u32[]{:S(2)}) %all-to-all-start.6) | async-done | bytes 917536 | tf_op jit(solution)/shard_map/all_to_all | solution.py:477
  823.0 8.5 fusion.208
  832.9 8.2 fusion.181
  842.4 3.7 fusion.171
  846.4 23.0 %all-reduce.16 = bf16[8,3,6]{2,1,0:T(4,128)(2,1)S(1)} all-reduce(bf16[8,3,6]{2,1,0:T(4,128)(2,1)S(1)} %broadcast_in_dim.350), channel_id=14, replica_groups=mesh['ctx'=8,'head'=4] {'ctx'}, use_global_device_ids=true, to_apply=%region_64.65.clone | all-reduce | flops 144 | bytes 576
  870.8 6.6 fusion.190
  877.5 38.4 %all-reduce.17 = (f32[1024]{0:T(1024)S(1)}, f32[1536]{0:T(1024)S(1)}, f32[1024]{0:T(1024)S(1)}, f32[1792,4]{0,1:T(4,128)S(1)}, f32[1792]{0:T(1024)S(1)}) all-reduce(f32[1024]{0:T(1024)S(1)} %get-tuple-element.2151, f32[1536]{0:T(1024)S(1)} %copy-done.66, ...), channel_id=9, replica_groups=mesh['ctx'=8,'head'=4] {'ctx','head'}, use_global_device_ids=true, to_apply=%region_51.52.clone | all-reduce | flops 12544 | bytes 100352
  919.8 174.5 %reduce-scatter.9.cloned.1.call-done = f32[32,4120]{1,0:T(8,128)} async-done(((f32[1024,4120]{1,0:T(8,128)}), f32[32,4120]{1,0:T(8,128)}) %reduce-scatter.9.cloned.1.call-update) | async-done | bytes 527376 | tf_op jit(solution)/shard_map/reduce_scatter | solution.py:519
  1094.4 184.9 %reduce-scatter.13.cloned.1.call-done = f32[32,4096]{1,0:T(8,128)} async-done(((f32[1024,4096]{1,0:T(8,128)}), f32[32,4096]{1,0:T(8,128)}) %reduce-scatter.13.cloned.1.call-update) | async-done | bytes 524304 | tf_op jit(solution)/shard_map/reduce_scatter | solution.py:521
  (621 shorter events, 258.8 us)
Async XLA Ops:
  7.2 90.3 %all-gather.12.cloned.1.call-start = ((), (), s32[]{:S(2)}) async-start(), calls=%async_computation.13 | async-start | bytes 8921088 | tf_op jit(solution)/shard_map/all_gather | solution.py:184
  54.8 49.7 %copy-start.44 = (f32[1024]{0:T(1024)}, f32[1024]{0:T(1024)S(1)}, u32[]{:S(2)}) copy-start(f32[1024]{0:T(1024)S(1)} %convert_element_type.225) | copy-start | bytes 12292
  95.8 94.8 %copy-start.64 = (f32[512]{0:T(512)}, f32[512]{0:T(512)S(1)}, u32[]{:S(2)}) copy-start(f32[512]{0:T(512)S(1)} %add_convert_fusion.2) | copy-start | bytes 6148
  104.5 144.9 %copy-start.13 = (bf16[128,4120]{0,1:T(8,128)(2,1)}, bf16[128,4120]{0,1:T(8,128)(2,1)S(1)}, u32[]{:S(2)}) copy-start(bf16[128,4120]{0,1:T(8,128)(2,1)S(1)} %convolution_convert_fusion) | copy-start | bytes 3164164
  105.4 7.0 all-to-all-start
  108.8 8.1 copy-start.82
  108.8 8.7 copy-start.76
  112.5 79.7 %copy-start.52 = (bf16[4,128,6]{1,2,0:T(8,128)(2,1)}, bf16[4,128,6]{1,2,0:T(8,128)(2,1)S(1)}, u32[]{:S(2)}) copy-start(bf16[4,128,6]{1,2,0:T(8,128)(2,1)S(1)} %all-to-all-done) | copy-start | bytes 18436
  112.5 17.3 %all-to-all-start.1 = ((bf16[4,128,896]{1,2,0:T(8,128)(2,1)}), bf16[4,128,896]{1,2,0:T(8,128)(2,1)}, u32[]{:S(2)}, u32[]{:S(2)}) async-start(bf16[4,128,896]{1,2,0:T(8,128)(2,1)} %pad_maximum_fusion.1), calls=%async_computation.1 | async-start | bytes 1835008 | tf_op jit(solution)/shard_map/all_to_all | solution.py:233
  116.7 100.1 %all-gather.14.cloned.1.call-start = ((), (), s32[]{:S(2)}) async-start(), calls=%async_computation.14 | async-start | bytes 1179648 | tf_op jit(solution)/shard_map/all_gather | solution.py:292
  116.8 73.8 %copy-start.78 = (f32[32]{0:T(128)}, f32[32]{0:T(128)S(1)}, u32[]{:S(2)}) copy-start(f32[32]{0:T(128)S(1)} %multiply_power_fusion) | copy-start | bytes 388
  116.9 19.6 %copy-start.55 = (f32[640]{0:T(1024)}, f32[640]{0:T(1024)S(1)}, u32[]{:S(2)}) copy-start(f32[640]{0:T(1024)S(1)} %get-tuple-element.2153) | copy-start | bytes 7684
  116.9 19.6 %copy-start.57 = (f32[640]{0:T(1024)}, f32[640]{0:T(1024)S(1)}, u32[]{:S(2)}) copy-start(f32[640]{0:T(1024)S(1)} %get-tuple-element.2154) | copy-start | bytes 7684
  116.9 19.6 %copy-start.59 = (f32[640]{0:T(1024)}, f32[640]{0:T(1024)S(1)}, u32[]{:S(2)}) copy-start(f32[640]{0:T(1024)S(1)} %get-tuple-element.2155) | copy-start | bytes 7684
  116.9 19.6 %copy-start.61 = (f32[640]{0:T(1024)}, f32[640]{0:T(1024)S(1)}, u32[]{:S(2)}) copy-start(f32[640]{0:T(1024)S(1)} %get-tuple-element.2156) | copy-start | bytes 7684
  131.7 3.5 collective-permute-start
  135.0 95.4 %all-gather.22.cloned.1.call-start = ((), (), s32[]{:S(2)}) async-start(), calls=%async_computation.23 | async-start | bytes 1769472 | tf_op jit(solution)/shard_map/all_gather | solution.py:32
  188.8 104.4 %all-gather.16.cloned.1.call-start = ((), (), s32[]{:S(2)}) async-start(), calls=%async_computation.15 | async-start | bytes 4325376 | tf_op jit(solution)/shard_map/all_gather | solution.py:185
  189.4 182.4 %all-gather.18.cloned.1.call-start = ((), (), s32[]{:S(2)}) async-start(), calls=%async_computation.16 | async-start | bytes 8650752 | tf_op jit(solution)/shard_map/all_gather | solution.py:186
  190.0 244.9 %all-gather.20.cloned.1.call-start = ((), (), s32[]{:S(2)}) async-start(), calls=%async_computation.17 | async-start | bytes 4325376 | tf_op jit(solution)/shard_map/all_gather | solution.py:187
  191.5 25.3 %copy-start.41 = (f32[512,32]{0,1:T(8,128)}, f32[512,32]{0,1:T(8,128)S(1)}, u32[]{:S(2)}) copy-start(f32[512,32]{0,1:T(8,128)S(1)} %get-tuple-element.2451) | copy-start | bytes 196612
  194.5 22.3 %copy-start.63 = (f32[1,6,4,128]{3,1,2,0:T(8,128)}, f32[1,6,4,128]{3,1,2,0:T(8,128)S(1)}, u32[]{:S(2)}) copy-start(f32[1,6,4,128]{3,1,2,0:T(8,128)S(1)} %copy.447) | copy-start | bytes 36868
  233.1 11.8 all-to-all-start.2
  238.7 11.7 copy-start.80
  238.8 10.7 copy-start.50
  238.8 55.1 %copy-start.19 = (bf16[128,1024]{1,0:T(8,128)(2,1)S(1)}, bf16[128,1024]{1,0:T(8,128)(2,1)}, u32[]{:S(2)}) copy-start(bf16[128,1024]{1,0:T(8,128)(2,1)} %param.30) | copy-start | bytes 786436
  244.9 48.4 %copy-start.15 = (bf16[4,128,384]{1,2,0:T(8,128)(2,1)}, bf16[4,128,384]{1,2,0:T(8,128)(2,1)S(1)}, u32[]{:S(2)}) copy-start(bf16[4,128,384]{1,2,0:T(8,128)(2,1)S(1)} %all-to-all-done.2) | copy-start | bytes 1179652
  244.9 48.4 %all-to-all-start.3 = ((bf16[4,128,128]{1,2,0:T(8,128)(2,1)}), bf16[4,128,128]{1,2,0:T(8,128)(2,1)S(1)}, u32[]{:S(2)}, u32[]{:S(2)}) async-start(bf16[4,128,128]{1,2,0:T(8,128)(2,1)} %copy.308), calls=%async_computation.3 | async-start | bytes 262144 | tf_op jit(solution)/shard_map/all_to_all | solution.py:331
  297.1 146.7 %copy-start.5 = (f32[128,1024]{1,0:T(8,128)}, f32[128,1024]{1,0:T(8,128)S(1)}, u32[]{:S(2)}) copy-start(f32[128,1024]{1,0:T(8,128)S(1)} %get-tuple-element.2464) | copy-start | bytes 1572868
  297.1 146.7 %copy-start.67 = (f32[128]{0:T(128)}, f32[128]{0:T(128)S(1)}, u32[]{:S(2)}) copy-start(f32[128]{0:T(128)S(1)} %get-tuple-element.2462) | copy-start | bytes 1540
  371.8 63.1 %copy-start.40 = (bf16[128,1024]{1,0:T(8,128)(2,1)S(1)}, bf16[128,1024]{1,0:T(8,128)(2,1)}, u32[]{:S(2)}) copy-start(bf16[128,1024]{1,0:T(8,128)(2,1)} %param.43) | copy-start | bytes 786436
  447.3 7.9 all-to-all-start.5
  450.6 341.8 %reduce-scatter.7.cloned.1.call-start = ((), (), s32[]{:S(2)}) async-start(), calls=%async_computation.18 | async-start | bytes 1179648 | tf_op jit(solution)/shard_map/reduce_scatter | solution.py:435
  467.6 452.2 %reduce-scatter.11.cloned.1.call-start = ((), (), s32[]{:S(2)}) async-start(), calls=%async_computation.20 | async-start | bytes 8650752 | tf_op jit(solution)/shard_map/reduce_scatter | solution.py:520
  473.5 84.6 %copy-start.1 = (f32[6,64,128]{2,1,0:T(8,128)S(1)}, f32[6,64,128]{2,1,0:T(8,128)}, u32[]{:S(2)}) copy-start(f32[6,64,128]{2,1,0:T(8,128)} %copy-done) | copy-start | bytes 589828
  606.5 14.8 %all-to-all-start.4 = ((bf16[128,4,384]{0,2,1:T(8,128)(2,1)}), bf16[128,4,384]{0,2,1:T(8,128)(2,1)S(1)}, u32[]{:S(2)}, u32[]{:S(2)}) async-start(bf16[128,4,384]{0,2,1:T(8,128)(2,1)} %bitcast.815), calls=%async_computation.4 | async-start | bytes 786432 | tf_op jit(solution)/shard_map/all_to_all | solution.py:380
  609.9 309.9 %reduce-scatter.15.cloned.1.call-start = ((), (), s32[]{:S(2)}) async-start(), calls=%async_computation.22 | async-start | bytes 8650752 | tf_op jit(solution)/shard_map/reduce_scatter | solution.py:522
  670.6 7.8 copy-start.7
  670.6 7.8 copy-start.73
  725.5 7.8 copy-start.7
  725.5 7.8 copy-start.73
  785.8 6.1 collective-permute-start.1
  788.6 7.2 all-to-all-start.7
  795.7 26.2 %all-to-all-start.6 = ((bf16[4,128,896]{1,2,0:T(8,128)(2,1)}), bf16[4,128,896]{1,2,0:T(8,128)(2,1)S(1)}, u32[]{:S(2)}, u32[]{:S(2)}) async-start(bf16[4,128,896]{1,2,0:T(8,128)(2,1)} %pad_maximum_fusion.2), calls=%async_computation.7 | async-start | bytes 1835008 | tf_op jit(solution)/shard_map/all_to_all | solution.py:477
  799.2 295.1 %reduce-scatter.9.cloned.1.call-start = ((), (), s32[]{:S(2)}) async-start(), calls=%async_computation.19 | async-start | bytes 17842176 | tf_op jit(solution)/shard_map/reduce_scatter | solution.py:519
  831.6 447.8 %reduce-scatter.13.cloned.1.call-start = ((), (), s32[]{:S(2)}) async-start(), calls=%async_computation.21 | async-start | bytes 17301504 | tf_op jit(solution)/shard_map/reduce_scatter | solution.py:521
  870.8 48.0 %copy-start.22 = (f32[128,1024]{1,0:T(8,128)S(1)}, f32[128,1024]{1,0:T(8,128)}, u32[]{:S(2)}) copy-start(f32[128,1024]{1,0:T(8,128)} %copy-done.21) | copy-start | bytes 1572868
  870.8 48.0 %copy-start.84 = (f32[128]{0:T(128)S(1)}, f32[128]{0:T(128)}, u32[]{:S(2)}) copy-start(f32[128]{0:T(128)} %get-tuple-element.2455) | copy-start | bytes 1540
  (71 other events, 204.2 us)
Sparse Core Ops, SparseCore 0:
  10.9 81.2 all-gather.11
  135.1 35.5 all-gather.13
  189.0 41.3 all-gather.21
  233.1 60.1 all-gather.15
  295.9 75.8 all-gather.17
  374.5 60.3 all-gather.19
  467.8 125.2 reduce-scatter.6
  595.9 151.1 reduce-scatter.10
  750.0 146.1 reduce-scatter.14
  903.0 191.2 reduce-scatter.8
  1097.2 182.0 reduce-scatter.12
where the time goes:
time: 1300 us; the launch traced here: 1290 us
  waiting for transfers between devices  598 us (46%)
  blocking collectives  278 us (21%)
  matrix products  142 us (11%)
  local copies, waits for them, and re-layouts  123 us (9%)
  other arithmetic  97 us (7%)
  starting transfers between devices  31.8 us (2%)
  between operations  15.8 us (1%)
    reduce_scatter x1, waiting for transfers between devices, on_device(): lax.psum_scatter(gu_grad, ('ctx', 'head'), scatter_dimension=0, tiled=True)  185 us
    reduce_scatter x1, waiting for transfers between devices, on_device(): lax.psum_scatter(in_grad, ('ctx', 'head'), scatter_dimension=0, tiled=True)  175 us
    all_gather x2, blocking collectives, carried_in(): lax.all_gather(part.astype(kind), axis)  115 us
    unnamed x3, blocking collectives  105 us
    all_gather x1, waiting for transfers between devices, on_device(): lax.all_gather(gu_weight, ('ctx', 'head'), axis=0, tiled=True)  74.7 us
    all_gather x1, waiting for transfers between devices, on_device(): lax.all_gather(down_weight, ('ctx', 'head'), axis=0, tiled=True)  57.1 us
    dynamic_update_slice x26, local copies, waits for them, and re-layouts, mixer_local(): lax.scan(advance, state, (shaped(inputs_x), shaped(bmat), shaped(cmat), s...  50.1 us
    all_gather x1, waiting for transfers between devices, on_device(): lax.all_gather(out_weight, ('ctx', 'head'), axis=0, tiled=True)  42.8 us
  transfers between devices with their start and end apart: 21, of which 13 were waited for; matrix products, arithmetic and copies ran while one was open for 25% of the time, Pallas kernels for 0%

commit v1 on v0

v1 whole, which is shorter than its diff:
```python
import math

import jax
import jax.numpy as jnp
from jax import lax
from jax.sharding import PartitionSpec as P

FF = 2048
MH = 24
MP = 64
NS = 128
KW = 4
AH = 8
KVH = 2
HDIM = 64
CHUNK = 128


EPSILON = 1e-05
ROPE_BASE = 10000.0
PRECISE_MODE = lax.Precision.HIGHEST


def passed_along(block, axis, distance):
    devices = range(lax.axis_size(axis))
    route = [(i - distance, i) for i in devices if i - distance in devices]
    return lax.ppermute(block, axis, route)


def silu_grad(value):
    sigmoid = jax.nn.sigmoid(value)
    return sigmoid * (1.0 + value * (1.0 - sigmoid))


def rotate_pairs(values, positions, direction):
    half_dim = values.shape[-1] // 2
    inverse = ROPE_BASE ** (-jnp.arange(half_dim).astype(jnp.float32) / half_dim)
    angles = positions[:, None] * inverse[None, :]
    cosine = jnp.cos(angles)[:, None, :]
    sine = direction * jnp.sin(angles)[:, None, :]
    first_half = values[..., :half_dim]
    second_half = values[..., half_dim:]
    return jnp.concatenate(
        [first_half * cosine - second_half * sine, second_half * cosine + first_half * sine],
        axis=-1,
    )


def dot_back(first_op, second_op):
    return lax.dot_general(
        first_op, second_op, (((1,), (1,)), ((), ())), preferred_element_type=jnp.float32
    )


def dot_rows(first_op, second_op):
    return lax.dot_general(
        first_op, second_op, (((0,), (0,)), ((), ())), preferred_element_type=jnp.float32
    )


def spread_to_all(block, axis):
    size = lax.axis_size(axis)
    copies = jnp.broadcast_to(block[None], (size,) + block.shape)
    return lax.all_to_all(copies, axis, split_axis=0, concat_axis=0, tiled=True)


def summed_parts(stacked, axis):
    got = lax.all_to_all(stacked, axis, split_axis=0, concat_axis=0, tiled=True)
    return jnp.sum(got.astype(jnp.float32), axis=0)


def ein(spec, first_op, second_op):
    return jnp.einsum(
        spec,
        first_op.astype(jnp.bfloat16),
        second_op.astype(jnp.bfloat16),
        preferred_element_type=jnp.float32,
    )


def on_device(
    x_in,
    in_weight,
    out_weight,
    gu_weight,
    down_weight,
    norm_gain,
    mixer_gain,
    ffn_gain,
    conv_weight,
    conv_bias,
    dt_bias,
    a_log,
    skip_gain,
    out_grad,
):
    f32 = jnp.float32
    half = jnp.bfloat16
    heads = lax.axis_size("head")
    ranges = lax.axis_size("ctx")
    ctx_place = lax.axis_index("ctx")
    head_place = lax.axis_index("head")
    tokens, width = x_in.shape
    rows = tokens * heads
    mix_heads = MH // heads
    attn_heads = AH // heads
    group_devices = heads // KVH
    dssm = MH * MP
    mine = mix_heads * MP
    local_cols = mine + 2 * NS
    qcols = attn_heads * HDIM
    rate_start = 2 * dssm + 2 * NS
    query_start = rate_start + MH
    key_start = query_start + AH * HDIM
    value_start = key_start + KVH * HDIM
    score_scale = 1.0 / math.sqrt(HDIM)
    count = rows // CHUNK
    w_rows = in_weight.shape[0]
    unit_rows = down_weight.shape[0]
    both = ("ctx", "head")

    def columns_for(target):
        kv = target // group_devices
        return jnp.concatenate(
            [
                in_weight[:, target * mine : (target + 1) * mine],
                in_weight[:, dssm + target * mine : dssm + (target + 1) * mine],
                in_weight[:, 2 * dssm : rate_start],
                in_weight[:, query_start + target * qcols : query_start + (target + 1) * qcols],
                in_weight[:, key_start + kv * HDIM : key_start + (kv + 1) * HDIM],
                in_weight[:, value_start + kv * HDIM : value_start + (kv + 1) * HDIM],
                in_weight[:, rate_start + target * mix_heads : rate_start + (target + 1) * mix_heads],
            ],
            axis=1,
        )

    in_parts = lax.all_to_all(
        jnp.stack([columns_for(target) for target in range(heads)]),
        "head",
        split_axis=0,
        concat_axis=0,
        tiled=True,
    ).reshape(heads * w_rows, -1)
    w_in = lax.all_gather(in_parts, "ctx", axis=0, tiled=True)
    x_all = spread_to_all(x_in, "head").reshape(rows, width)
    small = jnp.concatenate(
        [norm_gain, mixer_gain, ffn_gain, conv_weight.reshape(-1), conv_bias]
    )
    small_all = spread_to_all(small, both)
    cuts = [0]
    for piece in (norm_gain, mixer_gain, ffn_gain, conv_weight, conv_bias):
        cuts.append(cuts[-1] + piece.size)
    smalls = [small_all[:, cuts[i] : cuts[i + 1]].astype(f32) for i in range(5)]
    gain_one, gain_mix, gain_two = (smalls[i].reshape(-1) for i in range(3))
    conv_w = smalls[3].reshape(-1, KW)
    conv_b = smalls[4].reshape(-1)
    gu_split = gu_weight.reshape(w_rows, 2, ranges, heads, unit_rows)
    gu_parts = lax.all_to_all(
        gu_split.transpose(3, 0, 1, 2, 4).reshape(heads, w_rows, -1),
        "head",
        split_axis=0,
        concat_axis=0,
        tiled=True,
    ).reshape(heads * w_rows, -1)
    w_out = lax.all_gather(out_weight, both, axis=0, tiled=True)
    w_gu = lax.all_gather(gu_parts, "ctx", axis=0, tiled=True)
    w_down = lax.all_gather(down_weight, "ctx", axis=0, tiled=True)
    units = ranges * unit_rows

    inputs_all = x_all.astype(f32)
    rms_all = lax.rsqrt(jnp.mean(inputs_all * inputs_all, axis=1, keepdims=True) + EPSILON)
    normed = (inputs_all * rms_all * gain_one[None, :]).astype(half)
    proj = jnp.dot(normed, w_in, preferred_element_type=f32).astype(half)
    z_part = proj[:, :mine].astype(f32)
    xbc = proj[:, mine : mine + local_cols]
    at = mine + local_cols
    queries_raw = proj[:, at : at + qcols]
    keys_raw = proj[:, at + qcols : at + qcols + HDIM]
    values_raw = proj[:, at + qcols + HDIM : at + qcols + 2 * HDIM]
    rate_raw = proj[:, at + qcols + 2 * HDIM :]

    query_first = ctx_place * rows
    positions = (query_first + jnp.arange(rows)).astype(f32)
    q_rot = rotate_pairs(
        queries_raw.astype(f32).reshape(rows, attn_heads, HDIM), positions, 1.0
    ).astype(half)
    q_rows = q_rot.transpose(1, 0, 2).reshape(attn_heads * rows, HDIM)
    k_rot = (
        rotate_pairs(keys_raw.astype(f32).reshape(rows, 1, HDIM), positions, 1.0)
        .reshape(rows, HDIM)
        .astype(half)
    )
    kv_own = jnp.concatenate([k_rot, values_raw], axis=1)
    kv_all = spread_to_all(kv_own, "ctx")

    rim = passed_along(xbc[rows - (KW - 1) :], "ctx", 1)
    padded = jnp.concatenate([rim, xbc], axis=0).astype(f32)
    own_w = jnp.concatenate(
        [lax.dynamic_slice_in_dim(conv_w, head_place * mine, mine, 0), conv_w[dssm:]], axis=0
    )
    own_b = jnp.concatenate(
        [lax.dynamic_slice_in_dim(conv_b, head_place * mine, mine, 0), conv_b[dssm:]], axis=0
    )
    conv_pre = jnp.broadcast_to(own_b[None, :], (rows, local_cols))
    for offset in range(KW):
        conv_pre = conv_pre + padded[offset : offset + rows] * own_w[:, offset][None, :]
    conv_out = jax.nn.silu(conv_pre).astype(half)

    def by_chunk(value):
        return value.reshape(count, CHUNK, mix_heads, -1).transpose(0, 2, 1, 3)

    def from_chunk(value):
        return value.transpose(0, 2, 1, 3).reshape(rows, -1)

    mix_x = by_chunk(conv_out[:, :mine])
    bmat = conv_out[:, mine : mine + NS].reshape(count, CHUNK, NS)
    cmat = conv_out[:, mine + NS :].reshape(count, CHUNK, NS)
    dt_pre = (rate_raw.astype(f32) + dt_bias[None, :]).reshape(count, CHUNK, mix_heads)
    dt_pre = dt_pre.transpose(0, 2, 1)
    step = jax.nn.softplus(dt_pre)
    decay_rate = -jnp.exp(a_log)
    lower = jnp.arange(CHUNK)[:, None] >= jnp.arange(CHUNK)[None, :]
    tril = lower.astype(f32)
    cum = jnp.einsum(
        "nhs,ts->nht", step * decay_rate[None, :, None], tril, precision=PRECISE_MODE
    )
    within = jnp.exp(jnp.where(lower, cum[:, :, :, None] - cum[:, :, None, :], -jnp.inf))
    products = ein("ntm,nsm->nts", cmat, bmat)
    mixing = (products[:, None] * within * step[:, :, None, :]).astype(half)
    intra = ein("nhts,nhsp->nhtp", mixing, mix_x)
    x_f = mix_x.astype(f32)
    fade = jnp.exp(cum[:, :, -1:] - cum)
    reach = fade * step
    x_reach = (x_f * reach[..., None]).astype(half)
    ends = ein("nhsp,nsm->nhpm", x_reach, bmat)
    chunk_decay = jnp.exp(cum[:, :, -1])
    range_end = ends[0]
    range_decay = chunk_decay[0]
    for k in range(1, count):
        range_end = chunk_decay[k][:, None, None] * range_end + ends[k]
        range_decay = range_decay * chunk_decay[k]
    packed = jnp.concatenate(
        [range_end, jnp.broadcast_to(range_decay[:, None, None], (mix_heads, 8, NS))], axis=1
    )
    gathered = spread_to_all(packed, "ctx")
    decays = gathered[:, :, MP, 0]

    def weights(order, reached):
        factor = jnp.ones((mix_heads,), f32)
        found = [None] * ranges
        for j in order:
            found[j] = jnp.where(reached(j), factor, 0.0)
            factor = jnp.where(reached(j), factor * decays[j], factor)
        return jnp.stack(found)

    before = weights(range(ranges - 1, -1, -1), lambda j: j < ctx_place)
    after = weights(range(ranges), lambda j: j > ctx_place)
    states = [jnp.sum(before[:, :, None, None] * gathered[:, :, :MP], axis=0)]
    for k in range(count - 1):
        states.append(chunk_decay[k][:, None, None] * states[k] + ends[k])
    state = jnp.stack(states)
    grown = jnp.exp(cum)
    inter = ein("ntm,nhpm->nhtp", cmat, state) * grown[..., None]
    ssm_full = intra + inter + skip_gain[None, :, None, None] * x_f
    ssm_out = from_chunk(ssm_full.astype(half)).astype(f32)
    gated_mine = (ssm_out * jax.nn.silu(z_part)).astype(half)

    causal = jnp.arange(rows)[:, None] >= jnp.arange(rows)[None, :]
    causal = jnp.concatenate([causal] * attn_heads, axis=0)

    def key_block(number):
        piece = lax.dynamic_index_in_dim(kv_all, number, 0, False)
        return (piece[:, :HDIM], piece[:, HDIM:])

    scores = jnp.where(causal, dot_back(q_rows, k_rot) * score_scale, -jnp.inf)
    peak = jnp.max(scores, axis=1, keepdims=True)
    weight = jnp.exp(scores - peak)
    mass = jnp.sum(weight, axis=1, keepdims=True)
    total = jnp.dot(weight.astype(half), values_raw, preferred_element_type=f32)

    def attend(number, carry):
        peak, mass, total = carry
        keys_blk, vals_blk = key_block(number)
        scores = dot_back(q_rows, keys_blk) * score_scale
        new_peak = jnp.maximum(peak, jnp.max(scores, axis=1, keepdims=True))
        weight = jnp.exp(scores - new_peak)
        shrink = jnp.exp(peak - new_peak)
        mass = mass * shrink + jnp.sum(weight, axis=1, keepdims=True)
        total = total * shrink + jnp.dot(
            weight.astype(half), vals_blk, preferred_element_type=f32
        )
        return (new_peak, mass, total)

    peak, mass, total = lax.fori_loop(0, ctx_place, attend, (peak, mass, total))
    log_total = peak + jnp.log(mass)
    attn_rows = (total / mass).astype(half)
    attn_mine = attn_rows.reshape(attn_heads, rows, HDIM).transpose(1, 0, 2).reshape(rows, qcols)

    mixed_parts = lax.all_to_all(
        jnp.concatenate([gated_mine, attn_mine], axis=1).reshape(heads, tokens, -1),
        "head",
        split_axis=0,
        concat_axis=0,
        tiled=True,
    )
    gated = mixed_parts[:, :, :mine].transpose(1, 0, 2).reshape(tokens, dssm).astype(f32)
    attn_tok = mixed_parts[:, :, mine:].transpose(1, 0, 2).reshape(tokens, AH * HDIM)
    inputs = x_in.astype(f32)
    rms_in = lax.rsqrt(jnp.mean(inputs * inputs, axis=1, keepdims=True) + EPSILON)
    rms_mix = lax.rsqrt(jnp.mean(gated * gated, axis=1, keepdims=True) + EPSILON)
    mixed_norm = (gated * rms_mix * gain_mix[None, :]).astype(half)
    joined = jnp.concatenate([mixed_norm, attn_tok], axis=1)
    residual = inputs + jnp.dot(joined, w_out, preferred_element_type=f32)
    rms_ffn = lax.rsqrt(jnp.mean(residual * residual, axis=1, keepdims=True) + EPSILON)
    normed_ffn = (residual * rms_ffn * gain_two[None, :]).astype(half)
    normed_two = spread_to_all(normed_ffn, "head").reshape(rows, width)
    grad_all = spread_to_all(out_grad, "head").reshape(rows, width)
    gate_up = jnp.dot(normed_two, w_gu, preferred_element_type=f32)
    gate_part = gate_up[:, :units]
    up_part = gate_up[:, units:]
    activ = (jax.nn.silu(gate_part) * up_part).astype(half)
    d_activ = dot_back(grad_all, w_down)
    d_gate_up = jnp.concatenate(
        [d_activ * up_part * silu_grad(gate_part), d_activ * jax.nn.silu(gate_part)], axis=1
    ).astype(half)
    d_normed_ffn = summed_parts(
        dot_back(d_gate_up, w_gu).astype(half).reshape(heads, tokens, width), "head"
    )
    down_sum = lax.psum_scatter(
        dot_rows(activ, grad_all).astype(half), "ctx", scatter_dimension=0, tiled=True
    ).astype(f32)
    gu_sum = lax.psum_scatter(
        dot_rows(normed_two, d_gate_up).astype(half), "ctx", scatter_dimension=0, tiled=True
    )
    y_out = (
        residual
        + summed_parts(
            jnp.dot(activ, w_down, preferred_element_type=f32)
            .astype(half)
            .reshape(heads, tokens, width),
            "head",
        )
    ).astype(half)
    ffn_gain_grad = jnp.sum(d_normed_ffn * residual * rms_ffn, axis=0)
    scaled_ffn = gain_two[None, :] * d_normed_ffn
    d_residual = (
        out_grad.astype(f32)
        + rms_ffn * scaled_ffn
        - residual * rms_ffn**3 * jnp.mean(scaled_ffn * residual, axis=1, keepdims=True)
    )
    d_res_half = d_residual.astype(half)
    d_joined = dot_back(d_res_half, w_out)
    out_sum = lax.psum_scatter(
        dot_rows(joined, d_res_half).astype(half), both, scatter_dimension=0, tiled=True
    ).astype(f32)
    d_mixed = d_joined[:, :dssm]
    mixer_gain_grad = jnp.sum(d_mixed * gated * rms_mix, axis=0)
    scaled_mix = gain_mix[None, :] * d_mixed
    d_gated_tok = rms_mix * scaled_mix - gated * rms_mix**3 * jnp.mean(
        scaled_mix * gated, axis=1, keepdims=True
    )
    back_parts = jnp.concatenate(
        [
            d_gated_tok.astype(half).reshape(tokens, heads, mine),
            d_joined[:, dssm:].astype(half).reshape(tokens, heads, qcols),
        ],
        axis=2,
    ).transpose(1, 0, 2)
    back_got = lax.all_to_all(
        back_parts, "head", split_axis=0, concat_axis=0, tiled=True
    ).reshape(rows, mine + qcols)
    d_gated = back_got[:, :mine].astype(f32)
    d_z = d_gated * ssm_out * silu_grad(z_part)
    d_ssm = by_chunk((d_gated * jax.nn.silu(z_part)).astype(half))

    d_grown = (d_ssm.astype(f32) * grown[..., None]).astype(half)
    pulls = ein("nhtp,ntm->nhpm", d_grown, cmat)
    range_pull = pulls[count - 1]
    for k in range(count - 2, -1, -1):
        range_pull = chunk_decay[k][:, None, None] * range_pull + pulls[k]
    pulls_all = spread_to_all(range_pull.astype(half), "ctx").astype(f32)
    d_ends = [None] * count
    d_ends[count - 1] = jnp.sum(after[:, :, None, None] * pulls_all, axis=0)
    for k in range(count - 1, 0, -1):
        d_ends[k - 1] = chunk_decay[k][:, None, None] * d_ends[k] + pulls[k]
    d_end = jnp.stack(d_ends)

    d_rows = back_got[:, mine:].reshape(rows, attn_heads, HDIM).transpose(1, 0, 2)
    d_rows = d_rows.reshape(attn_heads * rows, HDIM)
    row_delta = jnp.sum(d_rows.astype(f32) * attn_rows.astype(f32), axis=1, keepdims=True)

    def back_block(scores, keys_blk, vals_blk):
        probs = jnp.exp(scores - log_total)
        d_probs = dot_back(d_rows, vals_blk)
        d_scores = (probs * (d_probs - row_delta)).astype(half)
        query_part = jnp.dot(d_scores, keys_blk, preferred_element_type=f32)
        key_part = dot_rows(d_scores, q_rows) * score_scale
        value_part = dot_rows(probs.astype(half), d_rows)
        return (query_part, jnp.concatenate([key_part, value_part], axis=1).astype(half))

    own_scores = jnp.where(causal, dot_back(q_rows, k_rot) * score_scale, -jnp.inf)
    query_grad, kv_own_grad = back_block(own_scores, k_rot, values_raw)

    def back_step(number, carry):
        query_grad, kv_grads = carry
        keys_blk, vals_blk = key_block(number)
        query_part, kv_part = back_block(
            dot_back(q_rows, keys_blk) * score_scale, keys_blk, vals_blk
        )
        kv_grads = lax.dynamic_update_index_in_dim(kv_grads, kv_part, number, 0)
        return (query_grad + query_part, kv_grads)

    kv_start = lax.dynamic_update_index_in_dim(
        jnp.zeros((ranges, rows, 2 * HDIM), half), kv_own_grad, ctx_place, 0
    )
    query_grad, kv_grads = lax.fori_loop(0, ctx_place, back_step, (query_grad, kv_start))
    kv_mine = summed_parts(kv_grads, "ctx")
    query_grad = (query_grad * score_scale).reshape(attn_heads, rows, HDIM).transpose(1, 0, 2)
    d_query = rotate_pairs(query_grad, positions, -1.0).reshape(rows, qcols)
    d_key = rotate_pairs(kv_mine[:, None, :HDIM], positions, -1.0).reshape(rows, HDIM)
    d_value = kv_mine[:, HDIM:]

    d_f = d_ssm.astype(f32)
    overlap = ein("nhtp,nhsp->nhts", d_ssm, mix_x) * within
    weighted = overlap * step[:, :, None, :]
    d_products = jnp.sum(weighted, axis=1)
    felt = overlap * products[:, None]
    felt_sum = jnp.sum(felt, axis=2)
    grad_step = felt_sum
    d_cum = jnp.sum(felt * step[:, :, None, :], axis=3) - step * felt_sum
    grad_b = ein("nts,ntm->nsm", d_products, cmat)
    grad_c = ein("nts,nsm->ntm", d_products, bmat)
    grad_x = ein("nhts,nhtp->nhsp", mixing, d_ssm)
    d_cum = d_cum + jnp.sum(d_f * inter, axis=3)
    grad_c = grad_c + ein("nhtp,nhpm->ntm", d_grown, state)
    d_reach_x = ein("nhpm,nsm->nhsp", d_end, bmat)
    grad_b = grad_b + ein("nhsp,nhpm->nsm", x_reach, d_end)
    grad_x = grad_x + reach[..., None] * d_reach_x + skip_gain[None, :, None, None] * d_f
    d_reach = jnp.sum(d_reach_x * x_f, axis=3)
    grad_step = grad_step + fade * d_reach
    moved = reach * d_reach
    last = jnp.sum(moved, axis=2) + chunk_decay * jnp.sum(d_end * state, axis=(2, 3))
    d_cum = d_cum - moved
    d_rate = jnp.einsum("nht,ts->nhs", d_cum, tril, precision=PRECISE_MODE) + last[:, :, None]
    grad_step = grad_step + d_rate * decay_rate[None, :, None]
    grad_decay = jnp.sum(d_rate * step, axis=(0, 2))
    skip_part = jnp.sum(d_f * x_f, axis=(0, 2, 3))
    d_dt_pre = grad_step * jax.nn.sigmoid(dt_pre)
    head_local = jnp.concatenate(
        [jnp.sum(d_dt_pre, axis=(0, 2)), grad_decay * decay_rate, skip_part]
    )
    d_rates = d_dt_pre.transpose(0, 2, 1).reshape(rows, mix_heads)

    d_conv_pre = jnp.concatenate(
        [from_chunk(grad_x), grad_b.reshape(rows, NS), grad_c.reshape(rows, NS)], axis=1
    ) * silu_grad(conv_pre)
    conv_b_local = jnp.sum(d_conv_pre, axis=0)
    conv_w_local = jnp.stack(
        [jnp.sum(d_conv_pre * padded[offset : offset + rows], axis=0) for offset in range(KW)],
        axis=1,
    )
    edge = passed_along(d_conv_pre[: KW - 1], "ctx", -1)
    d_long = jnp.concatenate([d_conv_pre, edge], axis=0)
    d_xbc = jnp.zeros((rows, local_cols), f32)
    for offset in range(KW):
        shift = KW - 1 - offset
        d_xbc = d_xbc + d_long[shift : shift + rows] * own_w[:, offset][None, :]
    d_proj = jnp.concatenate(
        [d_z, d_xbc, d_query, d_key, d_value, d_rates], axis=1
    ).astype(half)
    in_grad = dot_rows(normed, d_proj).astype(half)
    in_mine = summed_parts(in_grad.reshape(ranges, heads * w_rows, -1), "ctx").astype(half)
    d_normed = summed_parts(
        dot_back(d_proj, w_in).astype(half).reshape(heads, tokens, width), "head"
    )
    norm_gain_grad = jnp.sum(d_normed * inputs * rms_in, axis=0)
    scaled_in = gain_one[None, :] * d_normed
    x_grad = (
        d_residual
        + rms_in * scaled_in
        - inputs * rms_in**3 * jnp.mean(scaled_in * inputs, axis=1, keepdims=True)
    )

    gu_got = lax.all_to_all(
        gu_sum.reshape(heads, w_rows, -1), "head", split_axis=0, concat_axis=0, tiled=True
    ).astype(f32)
    gate_sum = (
        gu_got.reshape(heads, w_rows, 2, ranges, unit_rows)
        .transpose(1, 2, 3, 0, 4)
        .reshape(w_rows, -1)
    )
    in_got = lax.all_to_all(
        in_mine.reshape(heads, w_rows, -1), "head", split_axis=0, concat_axis=0, tiled=True
    ).astype(f32)

    def side_by_side(first, cols):
        return in_got[:, :, first : first + cols].transpose(1, 0, 2).reshape(w_rows, heads * cols)

    def grouped(first):
        piece = in_got[:, :, first : first + HDIM].reshape(KVH, group_devices, w_rows, HDIM)
        return jnp.sum(piece, axis=1).transpose(1, 0, 2).reshape(w_rows, KVH * HDIM)

    input_sum = jnp.concatenate(
        [
            side_by_side(0, mine),
            side_by_side(mine, mine),
            jnp.sum(in_got[:, :, 2 * mine : at], axis=0),
            side_by_side(at + qcols + 2 * HDIM, mix_heads),
            side_by_side(at, qcols),
            grouped(at + qcols),
            grouped(at + qcols + HDIM),
        ],
        axis=1,
    )

    def placed_rows(local):
        full = jnp.zeros((dssm + 2 * NS,) + local.shape[1:], f32)
        full = lax.dynamic_update_slice_in_dim(full, local[:mine], head_place * mine, 0)
        return lax.dynamic_update_slice_in_dim(full, local[mine:], dssm, 0)

    devices = ranges * heads
    own_head = (jnp.arange(devices) % heads == head_place).astype(f32)
    small_grads = jnp.concatenate(
        [
            norm_gain_grad.reshape(devices, -1),
            mixer_gain_grad.reshape(devices, -1),
            ffn_gain_grad.reshape(devices, -1),
            placed_rows(conv_w_local).reshape(devices, -1),
            placed_rows(conv_b_local).reshape(devices, -1),
            own_head[:, None] * head_local[None, :],
        ],
        axis=1,
    )
    small_sum = jnp.sum(
        lax.all_to_all(small_grads, both, split_axis=0, concat_axis=0, tiled=True), axis=0
    )
    head_sums = small_sum[cuts[5] :].reshape(3, mix_heads)
    return (
        y_out,
        x_grad,
        input_sum,
        out_sum,
        gate_sum,
        down_sum,
        small_sum[cuts[0] : cuts[1]],
        small_sum[cuts[1] : cuts[2]],
        small_sum[cuts[2] : cuts[3]],
        small_sum[cuts[3] : cuts[4]].reshape(-1, KW),
        small_sum[cuts[4] : cuts[5]],
        head_sums[0],
        head_sums[1],
        head_sums[2],
    )


def solution(mesh):
    placed = (
        P(("ctx", "head"), None),
        P(("ctx", "head"), None),
        P(("ctx", "head"), None),
        P(("ctx", "head"), None),
        P(("ctx", "head"), None),
        P(("ctx", "head")),
        P(("ctx", "head")),
        P(("ctx", "head")),
        P(("ctx", "head"), None),
        P(("ctx", "head")),
        P("head"),
        P("head"),
        P("head"),
        P(("ctx", "head"), None),
    )
    return jax.shard_map(
        on_device,
        mesh=mesh,
        in_specs=placed,
        out_specs=(
            P(("ctx", "head"), None),
            P(("ctx", "head"), None),
            P(("ctx", "head"), None),
            P(("ctx", "head"), None),
            P(("ctx", "head"), None),
            P(("ctx", "head"), None),
            P(("ctx", "head")),
            P(("ctx", "head")),
            P(("ctx", "head")),
            P(("ctx", "head"), None),
            P(("ctx", "head")),
            P("head"),
            P("head"),
            P("head"),
        ),
        check_vma=False,
    )
```

time: 1300 us -> 610 us (0.47)
  waiting for transfers between devices: 598 us -> 250 us
  blocking collectives: 278 us -> 28.8 us
  matrix products: 142 us -> 62.9 us
  starting transfers between devices: 31.8 us -> 102 us
  local copies, waits for them, and re-layouts: 123 us -> 69.9 us
  other arithmetic: 97 us -> 67.1 us
    reduce_scatter x5 -> x3, waiting for transfers between devices: 360 us -> 0.02 us  [the longest x1 0.02 us: on_device(): lax.psum_scatter(dot_rows(activ, grad_all).astype(half), 'ctx', scatter_d...]
    all_gather x4 -> x0, blocking collectives: 174 us -> none  [the longest x2 115 us: carried_in(): lax.all_gather(part.astype(kind), axis)]
    all_to_all x8 -> x17, waiting for transfers between devices: 50.2 us -> 219 us  [the longest x6 104 us: spread_to_all(): return lax.all_to_all(copies, axis, split_axis=0, concat_axis=0, tiled=True)]
    all_gather x6 -> x4, waiting for transfers between devices: 186 us -> 20.2 us  [the longest x1 13.3 us: on_device(): w_in = lax.all_gather(in_parts, 'ctx', axis=0, tiled=True)]
    unnamed x3 -> x0, blocking collectives: 105 us -> none
    all_to_all x8 -> x17, starting transfers between devices: 28.3 us -> 97.7 us  [the longest x5 40.6 us: summed_parts(): got = lax.all_to_all(stacked, axis, split_axis=0, concat_axis=0, tiled=True)]
    dot_general x43 -> x20, matrix products: 96.6 us -> 28.5 us  [the longest x12 12.2 us: ein(): jnp.einsum(spec, first_op.astype(jnp.bfloat16), second_op.astype(jnp.bflo...]
    dynamic_update_slice x29 -> x4, local copies, waits for them, and re-layouts: 50.2 us -> 0.16 us  [the longest x2 0.14 us: placed_rows(): lax.dynamic_update_slice_in_dim(full, local[:mine], head_place * mine, 0)]
  transfers between devices with their start and end apart: 21 -> 26, of which waited for: 13 -> 19; matrix products, arithmetic and copies ran while one was open for 25% -> 30% of each run, Pallas kernels for 0% -> 0%
where the time goes in v1:
time: 610 us; the launch traced here: 599 us
  waiting for transfers between devices  250 us (41%)
  starting transfers between devices  102 us (17%)
  local copies, waits for them, and re-layouts  69.9 us (11%)
  other arithmetic  67.1 us (11%)
  matrix products  62.9 us (10%)
  blocking collectives  28.8 us (5%)
  between operations  17 us (3%)
    all_to_all x6, waiting for transfers between devices, spread_to_all(): return lax.all_to_all(copies, axis, split_axis=0, concat_axis=0, tiled=True)  104 us
    all_to_all x5, waiting for transfers between devices, summed_parts(): got = lax.all_to_all(stacked, axis, split_axis=0, concat_axis=0, tiled=True)  94.6 us
    all_to_all x5, starting transfers between devices, summed_parts(): got = lax.all_to_all(stacked, axis, split_axis=0, concat_axis=0, tiled=True)  40.6 us
    all_to_all x6, starting transfers between devices, spread_to_all(): return lax.all_to_all(copies, axis, split_axis=0, concat_axis=0, tiled=True)  25.9 us
    all_to_all x1, blocking collectives, spread_to_all(): return lax.all_to_all(copies, axis, split_axis=0, concat_axis=0, tiled=True)  17.6 us
    dot_general x6, matrix products, dot_rows(): lax.dot_general(first_op, second_op, (((0,), (0,)), ((), ())), preferred_...  17.4 us
    dot_general x6, matrix products, dot_back(): lax.dot_general(first_op, second_op, (((1,), (1,)), ((), ())), preferred_...  17 us
    all_gather x1, waiting for transfers between devices, on_device(): w_in = lax.all_gather(in_parts, 'ctx', axis=0, tiled=True)  13.3 us
  transfers between devices with their start and end apart: 26, of which 19 were waited for; matrix products, arithmetic and copies ran while one was open for 30% of the time, Pallas kernels for 0%

profile of v1, /device:TPU:0, one launch (start us, length us, event | category | flops | bytes accessed | tf_op | source)
XLA Modules:
  0.0 599.0 jit_solution(17062562403037597385)
XLA Ops:
  12.8 11.2 %all_to_all.103 = bf16[4,32,1286]{2,1,0:T(8,128)(2,1)} all-to-all(bf16[4,32,1286]{2,1,0:T(8,128)(2,1)S(1)} %pad_maximum_fusion.8), channel_id=1, replica_groups=mesh['ctx'=8,'head'=4] {'head'}, dimensions={0} | all-to-all | bytes 658432 | tf_op jit(solution)/shard_map/all_to_all | solution.py:137
  27.3 5.3 all-to-all-start
  36.0 4.0 all-to-all-done
  40.0 3.4 all-to-all-start.7
  43.6 5.8 all-to-all-done.7
  50.6 3.5 all-to-all-start.1
  55.9 12.6 %all-to-all-done.1 = bf16[4,128,1024]{2,1,0:T(8,128)(2,1)S(1)} async-done(((bf16[4,128,1024]{2,1,0:T(8,128)(2,1)}), bf16[4,128,1024]{2,1,0:T(8,128)(2,1)S(1)}, u32[]{:S(2)}, u32[]{:S(2)}) %all-to-all-start.1) | async-done | bytes 1048608 | tf_op jit(solution)/shard_map/all_to_all | solution.py:64
  69.1 13.3 %all-gather.5.cloned.1.call-done = bf16[1024,1286]{1,0:T(8,128)(2,1)} async-done(((bf16[128,1286]{1,0:T(8,128)(2,1)}), bf16[1024,1286]{1,0:T(8,128)(2,1)}) %all-gather.5.cloned.1.call-update) | async-done | bytes 2633744 | tf_op jit(solution)/shard_map/all_gather | solution.py:144
  82.5 3.4 convolution_convert_fusion.3
  88.0 3.2 collective-permute-start
  93.7 4.3 all-to-all-start.4
  111.3 18.0 %all-to-all-done.4 = bf16[8,512,128]{2,1,0:T(8,128)(2,1)} async-done(((bf16[8,512,128]{2,1,0:T(8,128)(2,1)}), bf16[8,512,128]{2,1,0:T(8,128)(2,1)}, u32[]{:S(2)}, u32[]{:S(2)}) %all-to-all-start.4) | async-done | bytes 1048608 | tf_op jit(solution)/shard_map/all_to_all | solution.py:64
  131.5 4.3 all-to-all-start.3
  139.5 48.1 %all-to-all-done.3 = f32[8,6,72,128]{3,2,1,0:T(8,128)} async-done(((f32[8,6,72,128]{3,2,1,0:T(8,128)}), f32[8,6,72,128]{3,2,1,0:T(8,128)}, u32[]{:S(2)}, u32[]{:S(2)}) %all-to-all-start.3) | async-done | bytes 1769504 | tf_op jit(solution)/shard_map/all_to_all | solution.py:64
  197.3 3.5 all-to-all-start.5
  202.9 6.7 %all-to-all-done.5 = bf16[4,128,512]{1,2,0:T(8,128)(2,1)S(1)} async-done(((bf16[4,128,512]{1,2,0:T(8,128)(2,1)}), bf16[4,128,512]{1,2,0:T(8,128)(2,1)S(1)}, u32[]{:S(2)}, u32[]{:S(2)}) %all-to-all-start.5) | async-done | bytes 524320 | tf_op jit(solution)/shard_map/all_to_all | solution.py:299
  216.6 3.2 multiply_reduce_fusion.17
  221.2 17.6 %all_to_all.104 = bf16[4,128,1024]{2,1,0:T(8,128)(2,1)} all-to-all(bf16[4,128,1024]{2,1,0:T(8,128)(2,1)S(1)} %broadcast_in_dim.88), channel_id=1, replica_groups=mesh['ctx'=8,'head'=4] {'head'}, dimensions={0} | all-to-all | bytes 2097152 | tf_op jit(solution)/shard_map/all_to_all | solution.py:64
  239.9 4.2 all-to-all-start.9
  244.2 4.5 fusion.199
  248.8 9.9 %all-to-all-done.9 = bf16[4,128,1024]{2,1,0:T(8,128)(2,1)} async-done(((bf16[4,128,1024]{2,1,0:T(8,128)(2,1)}), bf16[4,128,1024]{2,1,0:T(8,128)(2,1)}, u32[]{:S(2)}, u32[]{:S(2)}) %all-to-all-start.9) | async-done | bytes 1048608 | tf_op jit(solution)/shard_map/all_to_all | solution.py:64
  258.6 6.9 %all-gather.11.cloned.1.call-done = bf16[512,1024]{1,0:T(8,128)(2,1)} async-done(((bf16[64,1024]{1,0:T(8,128)(2,1)}), bf16[512,1024]{1,0:T(8,128)(2,1)}) %all-gather.11.cloned.1.call-update) | async-done | bytes 1048592 | tf_op jit(solution)/shard_map/all_gather | solution.py:167
  265.5 4.2 multiply_convert_fusion.5
  270.5 3.0 convolution_convert_fusion.7
  273.7 4.2 convolution_convert_fusion.6
  277.9 4.3 all-to-all-start.10
  282.2 4.1 convolution_convert_fusion.4
  287.5 3.1 convolution_convert_fusion.8
  290.6 6.0 %all-to-all-done.10 = bf16[4,128,1024]{2,1,0:T(8,128)(2,1)} async-done(((bf16[4,128,1024]{2,1,0:T(8,128)(2,1)}), bf16[4,128,1024]{2,1,0:T(8,128)(2,1)}, u32[]{:S(2)}, u32[]{:S(2)}) %all-to-all-start.10) | async-done | bytes 1048608 | tf_op jit(solution)/shard_map/all_to_all | solution.py:68
  296.6 4.4 all-to-all-start.8
  306.0 9.6 %all-to-all-done.8 = bf16[4,128,1024]{2,1,0:T(8,128)(2,1)} async-done(((bf16[4,128,1024]{2,1,0:T(8,128)(2,1)}), bf16[4,128,1024]{2,1,0:T(8,128)(2,1)}, u32[]{:S(2)}, u32[]{:S(2)}) %all-to-all-start.8) | async-done | bytes 1048608 | tf_op jit(solution)/shard_map/all_to_all | solution.py:68
  329.9 4.2 all-to-all-start.11
  338.1 4.2 convolution_convert_fusion.2
  358.7 4.2 all-to-all-start.12
  375.3 11.6 %all-to-all-done.12 = bf16[8,6,64,128]{3,2,1,0:T(8,128)(2,1)} async-done(((bf16[8,6,64,128]{3,2,1,0:T(8,128)(2,1)}), bf16[8,6,64,128]{3,2,1,0:T(8,128)(2,1)}, u32[]{:S(2)}, u32[]{:S(2)}) %all-to-all-start.12) | async-done | bytes 786464 | tf_op jit(solution)/shard_map/all_to_all | solution.py:64
  386.9 22.8 %all-to-all-start.13 = ((bf16[8,512,128]{1,2,0:T(8,128)(2,1)}), bf16[8,512,128]{1,2,0:T(8,128)(2,1)}, u32[]{:S(2)}, u32[]{:S(2)}) async-start(bf16[8,512,128]{1,2,0:T(8,128)(2,1)} %get-tuple-element.107), calls=%async_computation.13 | async-start | bytes 2097152 | tf_op jit(solution)/shard_map/all_to_all | solution.py:68
  418.1 3.2 multiply_reduce_fusion.9
  427.3 10.3 %collective-permute-done.1 = f32[3,640]{0,1:T(8,128)} collective-permute-done((f32[3,640]{0,1:T(8,128)}, f32[3,640]{0,1:T(8,128)}, u32[]{:S(2)}, u32[]{:S(2)}) %collective-permute-start.1) | collective-permute-done | bytes 7712 | tf_op jit(solution)/shard_map/ppermute | solution.py:27
  437.6 4.1 fusion.66
  445.4 5.1 convolution_convert_fusion.5
  450.6 4.8 all-to-all-start.14
  461.6 13.1 %all-to-all-done.14 = bf16[4,128,1024]{2,1,0:T(8,128)(2,1)S(1)} async-done(((bf16[4,128,1024]{2,1,0:T(8,128)(2,1)}), bf16[4,128,1024]{2,1,0:T(8,128)(2,1)S(1)}, u32[]{:S(2)}, u32[]{:S(2)}) %all-to-all-start.14) | async-done | bytes 1048608 | tf_op jit(solution)/shard_map/all_to_all | solution.py:68
  475.9 13.3 %all-to-all-start.18 = ((f32[32,1,410]{2,1,0:T(1,128)}), f32[32,1,410]{2,1,0:T(1,128)S(1)}, u32[]{:S(2)}, u32[]{:S(2)}) async-start(f32[32,1,410]{2,1,0:T(1,128)} %copy.413), calls=%async_computation.21 | async-start | bytes 131072 | tf_op jit(solution)/shard_map/all_to_all | solution.py:535
  493.0 3.7 all-to-all-done.18
  496.6 4.4 all-to-all-start.15
  502.7 65.9 %all-to-all-done.15 = bf16[8,128,1286]{1,2,0:T(8,128)(2,1)} async-done(((bf16[8,128,1286]{1,2,0:T(8,128)(2,1)}), bf16[8,128,1286]{1,2,0:T(8,128)(2,1)}, u32[]{:S(2)}, u32[]{:S(2)}) %all-to-all-start.15) | async-done | bytes 2633760 | tf_op jit(solution)/shard_map/all_to_all | solution.py:68
  568.7 3.4 all-to-all-start.17
  578.0 3.5 all-to-all-start.16
  (533 shorter events, 160.5 us)
Async XLA Ops:
  7.2 75.3 %all-gather.5.cloned.1.call-start = ((), (), s32[]{:S(2)}) async-start(), calls=%async_computation.22 | async-start | bytes 3244032 | tf_op jit(solution)/shard_map/all_gather | solution.py:144
  8.1 16.9 %copy-start.113 = (bf16[32]{0:T(256)(128)(2,1)S(1)}, bf16[32]{0:T(256)(128)(2,1)}, u32[]{:S(2)}) copy-start(bf16[32]{0:T(256)(128)(2,1)} %param.23) | copy-start | bytes 196
  8.1 16.9 %copy-start.114 = (bf16[48]{0:T(256)(128)(2,1)S(1)}, bf16[48]{0:T(256)(128)(2,1)}, u32[]{:S(2)}) copy-start(bf16[48]{0:T(256)(128)(2,1)} %param.24) | copy-start | bytes 292
  8.1 16.9 %copy-start.115 = (bf16[32]{0:T(256)(128)(2,1)S(1)}, bf16[32]{0:T(256)(128)(2,1)}, u32[]{:S(2)}) copy-start(bf16[32]{0:T(256)(128)(2,1)} %param.25) | copy-start | bytes 196
  8.1 16.9 %copy-start.116 = (bf16[56]{0:T(256)(128)(2,1)S(1)}, bf16[56]{0:T(256)(128)(2,1)}, u32[]{:S(2)}) copy-start(bf16[56]{0:T(256)(128)(2,1)} %param.27) | copy-start | bytes 340
  12.6 21.8 %copy-start.51 = (bf16[32,4096]{1,0:T(8,128)(2,1)S(1)}, bf16[32,4096]{1,0:T(8,128)(2,1)}, u32[]{:S(2)}) copy-start(bf16[32,4096]{1,0:T(8,128)(2,1)} %param.21) | copy-start | bytes 786436
  24.0 192.5 %all-gather.7.cloned.1.call-start = ((), (), s32[]{:S(2)}) async-start(), calls=%async_computation.23 | async-start | bytes 4325376 | tf_op jit(solution)/shard_map/all_gather | solution.py:165
  27.3 12.7 %all-to-all-start = ((bf16[32,2,196]{2,1,0:T(2,128)(2,1)}), bf16[32,2,196]{2,1,0:T(2,128)(2,1)S(1)}, u32[]{:S(2)}, u32[]{:S(2)}) async-start(bf16[32,2,196]{2,1,0:T(2,128)(2,1)} %reshape.1122), calls=%async_computation | async-start | bytes 65536 | tf_op jit(solution)/shard_map/all_to_all | solution.py:64
  32.6 59.3 %copy-start.102 = (f32[32]{0:T(128)}, f32[32]{0:T(128)S(1)}, u32[]{:S(2)}) copy-start(f32[32]{0:T(128)S(1)} %multiply_power_fusion) | copy-start | bytes 388
  32.7 59.3 %copy-start.81 = (f32[512]{0:T(512)}, f32[512]{0:T(512)S(1)}, u32[]{:S(2)}) copy-start(f32[512]{0:T(512)S(1)} %add_convert_fusion.3) | copy-start | bytes 6148
  40.0 9.4 %all-to-all-start.7 = ((bf16[4,32,1024]{2,1,0:T(8,128)(2,1)}), bf16[4,32,1024]{2,1,0:T(8,128)(2,1)S(1)}, u32[]{:S(2)}, u32[]{:S(2)}) async-start(bf16[4,32,1024]{2,1,0:T(8,128)(2,1)} %reshape.1043), calls=%async_computation.7 | async-start | bytes 524288 | tf_op jit(solution)/shard_map/all_to_all | solution.py:158
  43.5 43.4 %copy-start.111 = (f32[6]{0:T(128)}, f32[6]{0:T(128)S(1)}, u32[]{:S(2)}) copy-start(f32[6]{0:T(128)S(1)} %exponential_negate_fusion) | copy-start | bytes 76
  50.6 17.9 %all-to-all-start.1 = ((bf16[4,128,1024]{2,1,0:T(8,128)(2,1)}), bf16[4,128,1024]{2,1,0:T(8,128)(2,1)S(1)}, u32[]{:S(2)}, u32[]{:S(2)}) async-start(bf16[4,128,1024]{2,1,0:T(8,128)(2,1)} %broadcast_in_dim.76), calls=%async_computation.1 | async-start | bytes 2097152 | tf_op jit(solution)/shard_map/all_to_all | solution.py:64
  54.1 190.1 %all-gather.9.cloned.1.call-start = ((), (), s32[]{:S(2)}) async-start(), calls=%async_computation.24 | async-start | bytes 2359296 | tf_op jit(solution)/shard_map/all_gather | solution.py:166
  55.9 45.5 %copy-start.73 = (f32[640]{0:T(1024)}, f32[640]{0:T(1024)S(1)}, u32[]{:S(2)}) copy-start(f32[640]{0:T(1024)S(1)} %get-tuple-element.221) | copy-start | bytes 7684
  55.9 45.5 %copy-start.75 = (f32[640]{0:T(1024)}, f32[640]{0:T(1024)S(1)}, u32[]{:S(2)}) copy-start(f32[640]{0:T(1024)S(1)} %get-tuple-element.222) | copy-start | bytes 7684
  55.9 45.5 %copy-start.77 = (f32[640]{0:T(1024)}, f32[640]{0:T(1024)S(1)}, u32[]{:S(2)}) copy-start(f32[640]{0:T(1024)S(1)} %get-tuple-element.223) | copy-start | bytes 7684
  55.9 45.5 %copy-start.79 = (f32[640]{0:T(1024)}, f32[640]{0:T(1024)S(1)}, u32[]{:S(2)}) copy-start(f32[640]{0:T(1024)S(1)} %get-tuple-element.224) | copy-start | bytes 7684
  69.1 16.7 %copy-start.33 = (bf16[512,1024]{1,0:T(8,128)(2,1)}, bf16[512,1024]{1,0:T(8,128)(2,1)S(1)}, u32[]{:S(2)}) copy-start(bf16[512,1024]{1,0:T(8,128)(2,1)S(1)} %fusion.22) | copy-start | bytes 3145732
  69.1 17.7 %copy-start.99 = (f32[6]{0:T(128)S(1)}, f32[6]{0:T(128)}, u32[]{:S(2)}) copy-start(f32[6]{0:T(128)} %param.28) | copy-start | bytes 76
  88.0 12.1 %collective-permute-start = (bf16[3,640]{0,1:T(8,128)(2,1)}, bf16[3,640]{0,1:T(8,128)(2,1)}, u32[]{:S(2)}, u32[]{:S(2)}) collective-permute-start(bf16[3,640]{0,1:T(8,128)(2,1)} %slice.523), channel_id=1, source_target_pairs={{0,4},{4,8},{8,12},{12,16},{16,20},{20,24},{24,28},{1,5},{5,9},{9,... | collective-permute-start | bytes 11528 | tf_op jit(solution)/shard_map/ppermute | solution.py:27
  93.7 35.6 %all-to-all-start.4 = ((bf16[8,512,128]{2,1,0:T(8,128)(2,1)}), bf16[8,512,128]{2,1,0:T(8,128)(2,1)}, u32[]{:S(2)}, u32[]{:S(2)}) async-start(bf16[8,512,128]{2,1,0:T(8,128)(2,1)} %broadcast_in_dim.86), calls=%async_computation.4 | async-start | bytes 2097152 | tf_op jit(solution)/shard_map/all_to_all | solution.py:64
  131.5 56.0 %all-to-all-start.3 = ((f32[8,6,72,128]{3,2,1,0:T(8,128)}), f32[8,6,72,128]{3,2,1,0:T(8,128)}, u32[]{:S(2)}, u32[]{:S(2)}) async-start(f32[8,6,72,128]{3,2,1,0:T(8,128)} %broadcast_in_dim.80), calls=%async_computation.3 | async-start | bytes 3538944 | tf_op jit(solution)/shard_map/all_to_all | solution.py:64
  197.3 12.3 %all-to-all-start.5 = ((bf16[4,128,512]{1,2,0:T(8,128)(2,1)}), bf16[4,128,512]{1,2,0:T(8,128)(2,1)S(1)}, u32[]{:S(2)}, u32[]{:S(2)}) async-start(bf16[4,128,512]{1,2,0:T(8,128)(2,1)} %pad_maximum_fusion.6), calls=%async_computation.5 | async-start | bytes 1048576 | tf_op jit(solution)/shard_map/all_to_all | solution.py:299
  200.8 64.8 %all-gather.11.cloned.1.call-start = ((), (), s32[]{:S(2)}) async-start(), calls=%async_computation.25 | async-start | bytes 1179648 | tf_op jit(solution)/shard_map/all_gather | solution.py:167
  202.9 17.5 %copy-start.67 = (f32[1024]{0:T(1024)}, f32[1024]{0:T(1024)S(1)}, u32[]{:S(2)}) copy-start(f32[1024]{0:T(1024)S(1)} %reshape.1095) | copy-start | bytes 12292
  219.8 97.4 %copy-start.3 = (f32[128,1024]{1,0:T(8,128)}, f32[128,1024]{1,0:T(8,128)S(1)}, u32[]{:S(2)}) copy-start(f32[128,1024]{1,0:T(8,128)S(1)} %get-tuple-element.353) | copy-start | bytes 1572868
  221.1 17.7 %copy-start.36 = (bf16[128,1024]{1,0:T(8,128)(2,1)S(1)}, bf16[128,1024]{1,0:T(8,128)(2,1)}, u32[]{:S(2)}) copy-start(bf16[128,1024]{1,0:T(8,128)(2,1)} %param.31) | copy-start | bytes 786436
  239.9 18.7 %all-to-all-start.9 = ((bf16[4,128,1024]{2,1,0:T(8,128)(2,1)}), bf16[4,128,1024]{2,1,0:T(8,128)(2,1)}, u32[]{:S(2)}, u32[]{:S(2)}) async-start(bf16[4,128,1024]{2,1,0:T(8,128)(2,1)} %broadcast_in_dim.89), calls=%async_computation.9 | async-start | bytes 2097152 | tf_op jit(solution)/shard_map/all_to_all | solution.py:64
  244.1 257.0 %reduce-scatter.8.cloned.1.call-start = ((), (), s32[]{:S(2)}) async-start(), calls=%async_computation.28 | async-start | bytes 1179648 | tf_op jit(solution)/shard_map/reduce_scatter | solution.py:329
  277.9 18.8 %all-to-all-start.10 = ((bf16[4,128,1024]{2,1,0:T(8,128)(2,1)}), bf16[4,128,1024]{2,1,0:T(8,128)(2,1)}, u32[]{:S(2)}, u32[]{:S(2)}) async-start(bf16[4,128,1024]{2,1,0:T(8,128)(2,1)} %bitcast.563), calls=%async_computation.10 | async-start | bytes 2097152 | tf_op jit(solution)/shard_map/all_to_all | solution.py:68
  282.1 220.6 %reduce-scatter.6.cloned.1.call-start = ((), (), s32[]{:S(2)}) async-start(), calls=%async_computation.27 | async-start | bytes 2359296 | tf_op jit(solution)/shard_map/reduce_scatter | solution.py:332
  296.6 18.9 %all-to-all-start.8 = ((bf16[4,128,1024]{2,1,0:T(8,128)(2,1)}), bf16[4,128,1024]{2,1,0:T(8,128)(2,1)}, u32[]{:S(2)}, u32[]{:S(2)}) async-start(bf16[4,128,1024]{2,1,0:T(8,128)(2,1)} %bitcast.565), calls=%async_computation.8 | async-start | bytes 2097152 | tf_op jit(solution)/shard_map/all_to_all | solution.py:68
  329.9 13.0 %all-to-all-start.11 = ((bf16[4,128,512]{1,2,0:T(8,128)(2,1)}), bf16[4,128,512]{1,2,0:T(8,128)(2,1)}, u32[]{:S(2)}, u32[]{:S(2)}) async-start(bf16[4,128,512]{1,2,0:T(8,128)(2,1)} %maximum_bitcast_fusion), calls=%async_computation.11 | async-start | bytes 1048576 | tf_op jit(solution)/shard_map/all_to_all | solution.py:369
  334.1 256.0 %reduce-scatter.4.cloned.1.call-start = ((), (), s32[]{:S(2)}) async-start(), calls=%async_computation.26 | async-start | bytes 4325376 | tf_op jit(solution)/shard_map/reduce_scatter | solution.py:353
  358.7 28.2 %all-to-all-start.12 = ((bf16[8,6,64,128]{3,2,1,0:T(8,128)(2,1)}), bf16[8,6,64,128]{3,2,1,0:T(8,128)(2,1)}, u32[]{:S(2)}, u32[]{:S(2)}) async-start(bf16[8,6,64,128]{3,2,1,0:T(8,128)(2,1)} %broadcast_in_dim.91), calls=%async_computation.12 | async-start | bytes 1572864 | tf_op jit(solution)/shard_map/all_to_all | solution.py:64
  373.0 36.7 %copy-start.84 = (f32[8,6]{1,0:T(8,128)S(1)}, f32[8,6]{1,0:T(8,128)}, u32[]{:S(2)}) copy-start(f32[8,6]{1,0:T(8,128)} %stack.82) | copy-start | bytes 580
  375.3 36.0 %copy-start.10 = (f32[4,6,64,128]{3,2,1,0:T(8,128)S(1)}, f32[4,6,64,128]{3,2,1,0:T(8,128)}, u32[]{:S(2)}) copy-start(f32[4,6,64,128]{3,2,1,0:T(8,128)} %copy-done.9) | copy-start | bytes 2359300
  375.3 36.0 %copy-start.97 = (f32[6]{0:T(128)S(1)}, f32[6]{0:T(128)}, u32[]{:S(2)}) copy-start(f32[6]{0:T(128)} %get-tuple-element.332) | copy-start | bytes 76
  375.3 36.0 %copy-start.104 = (f32[6]{0:T(128)S(1)}, f32[6]{0:T(128)}, u32[]{:S(2)}) copy-start(f32[6]{0:T(128)} %get-tuple-element.333) | copy-start | bytes 76
  386.9 55.5 %all-to-all-start.13 = ((bf16[8,512,128]{1,2,0:T(8,128)(2,1)}), bf16[8,512,128]{1,2,0:T(8,128)(2,1)}, u32[]{:S(2)}, u32[]{:S(2)}) async-start(bf16[8,512,128]{1,2,0:T(8,128)(2,1)} %get-tuple-element.107), calls=%async_computation.13 | async-start | bytes 2097152 | tf_op jit(solution)/shard_map/all_to_all | solution.py:68
  423.2 14.4 %collective-permute-start.1 = (f32[3,640]{0,1:T(8,128)}, f32[3,640]{0,1:T(8,128)}, u32[]{:S(2)}, u32[]{:S(2)}) collective-permute-start(f32[3,640]{0,1:T(8,128)} %slice.576), channel_id=1, source_target_pairs={{4,0},{8,4},{12,8},{16,12},{20,16},{24,20},{28,24},{5,1},{9,5},{13... | collective-permute-start | bytes 23048 | tf_op jit(solution)/shard_map/ppermute | solution.py:27
  450.6 24.1 %all-to-all-start.14 = ((bf16[4,128,1024]{2,1,0:T(8,128)(2,1)}), bf16[4,128,1024]{2,1,0:T(8,128)(2,1)S(1)}, u32[]{:S(2)}, u32[]{:S(2)}) async-start(bf16[4,128,1024]{2,1,0:T(8,128)(2,1)} %bitcast.564), calls=%async_computation.14 | async-start | bytes 2097152 | tf_op jit(solution)/shard_map/all_to_all | solution.py:68
  475.9 20.7 %all-to-all-start.18 = ((f32[32,1,410]{2,1,0:T(1,128)}), f32[32,1,410]{2,1,0:T(1,128)S(1)}, u32[]{:S(2)}, u32[]{:S(2)}) async-start(f32[32,1,410]{2,1,0:T(1,128)} %copy.413), calls=%async_computation.21 | async-start | bytes 131072 | tf_op jit(solution)/shard_map/all_to_all | solution.py:535
  493.0 79.1 %copy-start.119 = (f32[128]{0:T(128)S(1)}, f32[128]{0:T(128)}, u32[]{:S(2)}) copy-start(f32[128]{0:T(128)} %get-tuple-element.338) | copy-start | bytes 1540
  496.6 72.0 %all-to-all-start.15 = ((bf16[8,128,1286]{1,2,0:T(8,128)(2,1)}), bf16[8,128,1286]{1,2,0:T(8,128)(2,1)}, u32[]{:S(2)}, u32[]{:S(2)}) async-start(bf16[8,128,1286]{1,2,0:T(8,128)(2,1)} %copy.400), calls=%async_computation.15 | async-start | bytes 5275648 | tf_op jit(solution)/shard_map/all_to_all | solution.py:68
  568.7 9.4 %all-to-all-start.17 = ((bf16[4,32,1024]{2,1,0:T(8,128)(2,1)}), bf16[4,32,1024]{2,1,0:T(8,128)(2,1)S(1)}, u32[]{:S(2)}, u32[]{:S(2)}) async-start(bf16[4,32,1024]{2,1,0:T(8,128)(2,1)} %bitcast.594), calls=%async_computation.19 | async-start | bytes 524288 | tf_op jit(solution)/shard_map/all_to_all | solution.py:484
  578.0 10.5 %all-to-all-start.16 = ((bf16[4,32,1286]{2,1,0:T(8,128)(2,1)}), bf16[4,32,1286]{2,1,0:T(8,128)(2,1)S(1)}, u32[]{:S(2)}, u32[]{:S(2)}) async-start(bf16[4,32,1286]{2,1,0:T(8,128)(2,1)} %bitcast.105), calls=%async_computation.16 | async-start | bytes 720896 | tf_op jit(solution)/shard_map/all_to_all | solution.py:492
  (106 other events, 505.1 us)
Sparse Core Ops, SparseCore 0:
  24.2 58.2 all-gather.4
  85.3 78.7 all-gather.6
  166.8 57.7 all-gather.8
  226.6 38.8 all-gather.10
  273.6 63.1 reduce-scatter.7
  340.2 74.9 reduce-scatter.5
  417.4 152.8 reduce-scatter.3
